TPU v7x, 32 devices: a whole 2x2x4 slice. The times are simulated.
32 devices in a mesh: tm: 4 (over z), query: 2 (over y), rec: 4 (over x, core).
Axes of the slice: x: 2, y: 2, z: 4, core: 2. Of those that a mesh axis runs over, the one named last changes fastest.
Arguments:
- frames: bfloat16 [4, 2048, 1024], P('rec', 'tm'), may hold values from -100 to 100
- queries: bfloat16 [4096, 1024], P('query'), may hold values from -10 to 10
- kernel: float32 [33, 4096], P(None, 'query'), may hold values from 0.01 to 0.12
- labels: int32 [4, 2048], P('rec', 'tm'), may hold values from 0 to 4095
- lengths: int32 [4], P('rec'), may hold values from 512 to 2048, as said below
Outputs:
- grad_frames: bfloat16 [4, 2048, 1024], P('rec', 'tm', 'query')
- grad_queries: bfloat16 [4096, 1024], P('query', 'rec')
- grad_kernel: float32 [33, 4096], P(None, 'query')
Inputs may be any that keep to these rules, and one draw needn't show every extreme that they name: `lengths`: each entry counts the valid frames at the start of its recording; at least one recording has all 2048 frames valid.
All inputs are finite; a program needn't handle non-finite values.
Results may differ from a plain program's by a relative error of at most 0.0049.
Values sent between devices are 32-bit elements; how exact they have to be, the bound alone decides.
A program may use at most 64 MiB of HBM per device.

v0:
```python
import functools
import math

import jax
import jax.numpy as jnp
from jax import lax
from jax.experimental import pallas as pl
from jax.experimental.pallas import tpu as pltpu
from jax.sharding import PartitionSpec as P


GROUPS = 4
LANES = 128


def spread_taps(kern_ref, lanes):
    taps = kern_ref.shape[0]
    return [jnp.broadcast_to(kern_ref[j : j + 1, lanes], (8, LANES)) for j in range(taps)]


def tap_block(load, taps, flipped):
    count = len(taps)
    sums = [None] * GROUPS
    for o in range(8 * (GROUPS - 1) + count):
        v = load(o)
        for i in range(GROUPS):
            j = o - 8 * i
            if 0 <= j < count:
                term = taps[count - 1 - j if flipped else j] * v
                sums[i] = term if sums[i] is None else sums[i] + term
    return sums


MESH = pl.DeviceIdType.MESH


def bit_reversed(p, bits):
    return sum(((p >> k) & 1) << (bits - 1 - k) for k in range(bits))


def gradient_kernel(
    dims,
    scale,
    own_lab_ref,
    len_ref,
    fr_ref,
    qu_ref,
    kern_ref,
    gf_ref,
    gq_ref,
    gk_ref,
    *scratch,
):
    tms, peers, recs, chunk = dims
    bits = recs.bit_length() - 1
    acc, scratch = scratch[:bits], scratch[bits:]
    arrived, scratch = scratch[:bits], scratch[bits:]
    kacc, scratch = scratch[:bits], scratch[bits:]
    karrived, scratch = scratch[:bits], scratch[bits:]
    (mid, outer, inner, kmid, kouter, kinner, fpart, fin, sg_ref, grad, ksum) = scratch[:11]
    (sc_ref, e_ref, f_ref, lab_ref, valid_ref, x_ref, hin, hout, stat, stat_in) = scratch[11:21]
    scratch = scratch[21:]
    (rec_send, rec_recv, in_send, out_recv, out_send, inn_recv, f_send, f_recv) = scratch[:8]
    (h_send, h_recv, s_send, s_recv) = scratch[8:]

    t = lax.axis_index("tm")
    y = lax.axis_index("query")
    r = lax.axis_index("rec")
    half = tms // 2
    low = t < half
    is_end = (t == 0) | (t == tms - 1)
    is_mid = (t == half - 1) | (t == half)
    inward = jnp.where(low, t + 1, t - 1)
    outward = jnp.where(low, lax.rem(t + tms - 1, tms), lax.rem(t + 1, tms))
    my_bits = [lax.rem(r // (1 << k), 2) for k in range(bits)]
    rec_peers = [r + (1 - 2 * my_bits[k]) * (1 << k) for k in range(bits)]

    barrier = pltpu.get_barrier_semaphore()

    def greet(device):
        pl.semaphore_signal(barrier, inc=1, device_id=device, device_id_type=MESH)

    for peer in rec_peers:
        greet({"rec": peer})
    for d in range(1, peers):
        greet({"query": lax.rem(y + d, peers)})
    greet({"tm": inward})

    @pl.when(jnp.logical_not(is_end))
    def _():
        greet({"tm": outward})

    pl.semaphore_wait(barrier, jnp.where(is_end, bits + peers, bits + peers + 1))

    queries, width = (qu_ref.shape[0], fr_ref.shape[1])
    count = queries // chunk
    cols = width // recs
    fcols = width // peers
    row_count = sg_ref.shape[0]

    def copy(src, dst, send, recv, device):
        return pltpu.make_async_remote_copy(
            src_ref=src,
            dst_ref=dst,
            send_sem=send,
            recv_sem=recv,
            device_id=device,
            device_id_type=MESH,
        )

    def at(c):
        return pl.ds(pl.multiple_of(c * chunk, chunk), chunk)

    def f_copy(d):
        p = lax.rem(y + d, peers)
        return copy(fpart.at[p], fin.at[d - 1], f_send.at[d - 1], f_recv.at[d - 1], {"query": p})

    def f_compute(p):
        tile = 128
        columns = pl.ds(pl.multiple_of(p * fcols, fcols), fcols)

        def body(i, carry):
            rows = pl.ds(pl.multiple_of(i * tile, tile), tile)
            fpart[p, rows, :] = jnp.dot(
                sg_ref[rows, :], qu_ref[:, columns], preferred_element_type=jnp.float32
            )
            return carry

        lax.fori_loop(0, row_count // tile, body, 0)

    def rec_copies(k, c):
        n = recs >> k
        theirs = (1 - my_bits[k]) * (n // 2)
        device = {"rec": rec_peers[k]}
        return (
            copy(
                acc[k].at[pl.ds(theirs, n // 2), at(c)],
                arrived[k].at[:, at(c)],
                rec_send.at[k, 0, c],
                rec_recv.at[k, 0, c],
                device,
            ),
            copy(
                kacc[k].at[c],
                karrived[k].at[c],
                rec_send.at[k, 1, c],
                rec_recv.at[k, 1, c],
                device,
            ),
        )

    def summed(k, c):
        for one in rec_copies(k, c):
            one.wait_recv()
        n = recs >> k
        mine = my_bits[k] * (n // 2)
        total = acc[k][pl.ds(mine, n // 2), at(c), :] + arrived[k][:, at(c), :]
        return total, kacc[k][c] + karrived[k][c]

    def inward_copies(c, to_mid):
        big, small = (inner, kinner) if to_mid else (outer, kouter)
        recv = inn_recv if to_mid else out_recv
        device = {"tm": inward}
        return (
            copy(mid.at[at(c)], big.at[at(c)], in_send.at[0, c], recv.at[0, c], device),
            copy(kmid.at[c], small.at[c], in_send.at[1, c], recv.at[1, c], device),
        )

    def outward_copies(c):
        device = {"tm": outward}
        return (
            copy(inner.at[at(c)], inner.at[at(c)], out_send.at[0, c], inn_recv.at[0, c], device),
            copy(kinner.at[c], kinner.at[c], out_send.at[1, c], inn_recv.at[1, c], device),
        )

    taps_n = kern_ref.shape[0]
    rim = taps_n // 2
    halo = 2 * rim
    block = 8 * GROUPS
    ext = grad.shape[0]
    tiles = e_ref.shape[0]
    wide = x_ref.shape[0]
    lane = lax.broadcasted_iota(jnp.int32, (8, LANES), 1) + y * queries

    def halo_copy(side):
        device = {"tm": lax.rem(t + (tms - 1 if side == 0 else 1), tms)}
        return copy(
            hout.at[side], hin.at[1 - side], h_send.at[side], h_recv.at[1 - side], device
        )

    for side, begin in enumerate((0, row_count - halo)):
        rows = slice(begin, begin + halo)
        hout[side, :, :width] = fr_ref[rows, :].astype(jnp.float32)
        hout[side, :, width:] = own_lab_ref[rows, :].astype(jnp.float32)

    has = [t > 0, t < tms - 1]
    for side in range(2):
        @pl.when(has[side])
        def _(side=side):
            halo_copy(side).start()

    frame = lax.broadcasted_iota(jnp.int32, (wide, LANES), 0) + (t * row_count - halo)
    valid_ref[...] = jnp.where((frame >= 0) & (frame < len_ref[0]), 1.0, 0.0)
    x_ref[halo : halo + row_count, :] = fr_ref[...]
    lab_ref[rim : rim + row_count, :] = own_lab_ref[...].astype(jnp.float32)
    stat[...] = jnp.zeros_like(stat)
    f_ref[...] = jnp.full_like(f_ref, -jnp.inf)

    for side in range(2):
        @pl.when(has[side])
        def _(side=side):
            halo_copy(1 - side).wait_recv()

        @pl.when(jnp.logical_not(has[side]))
        def _(side=side):
            hin[side] = jnp.zeros((halo, hin.shape[2]), jnp.float32)

    x_ref[:halo, :] = hin[0, :, :width].astype(jnp.bfloat16)
    x_ref[halo + row_count :, :] = hin[1, :, :width].astype(jnp.bfloat16)
    lab_ref[:rim, :] = hin[0, halo - rim :, width:]
    lab_ref[rim + row_count :, :] = hin[1, :rim, width:]

    def score(c, carry):
        rows = pl.ds(pl.multiple_of(c * 2 * LANES, 2 * LANES), 2 * LANES)
        part = lax.dot_general(
            x_ref[...],
            qu_ref[rows, :],
            (((1,), (1,)), ((), ())),
            preferred_element_type=jnp.float32,
        )
        for h in range(2):
            one = part[:, h * LANES : (h + 1) * LANES] * scale
            sc_ref[2 * c + h] = jnp.where(valid_ref[...] > 0, one, 0.0)
        return carry

    lax.fori_loop(0, tiles // 2, score, 0)

    def smoothed(c, carry):
        taps = spread_taps(kern_ref, at(c))

        def body(g, carry):
            base = pl.multiple_of(g * block, block)
            sums = tap_block(lambda o: sc_ref[c, pl.ds(base + o, 8), :], taps, False)
            for i in range(GROUPS):
                rows = pl.ds(base + 8 * i, 8)
                e_ref[c, rows, :] = sums[i]
                f_ref[rows, :] = jnp.maximum(f_ref[rows, :], sums[i])
            return carry

        return lax.fori_loop(0, ext // block, body, carry)

    lax.fori_loop(0, tiles, smoothed, 0)

    diagonal = lax.broadcasted_iota(jnp.int32, (block, LANES), 0) == lax.broadcasted_iota(
        jnp.int32, (block, LANES), 1
    )

    def finish(g, carry):
        rows = pl.ds(pl.multiple_of(g * block, block), block)
        top = jnp.max(f_ref[rows, :], axis=1, keepdims=True)
        top = jnp.broadcast_to(top, (block, LANES))
        total = jnp.zeros((block, LANES), jnp.float32)
        for c in range(tiles):
            e = jnp.exp(e_ref[c, rows, :] - top)
            e_ref[c, rows, :] = e
            total = total + e
        total = jnp.broadcast_to(jnp.sum(total, axis=1, keepdims=True), (block, LANES))
        for i, value in enumerate((top, total)):
            picked = jnp.where(diagonal, value, 0.0)
            stat[0, i, pl.ds(g, 1), :] = jnp.sum(picked, axis=0, keepdims=True)
        return carry

    lax.fori_loop(0, ext // block, finish, 0)

    def stat_copy(k):
        bit = lax.rem(y // (1 << k), 2)
        device = {"query": y + (1 - 2 * bit) * (1 << k)}
        return copy(stat.at[k], stat_in.at[k], s_send.at[k], s_recv.at[k], device)

    rounds = peers.bit_length() - 1
    for k in range(rounds):
        stat_copy(k).start()
        stat_copy(k).wait_recv()
        top = jnp.maximum(stat[k, 0], stat_in[k, 0])
        stat[k + 1, 0] = top
        stat[k + 1, 1] = stat[k, 1] * jnp.exp(stat[k, 0] - top) + stat_in[k, 1] * jnp.exp(
            stat_in[k, 0] - top
        )
    stat[rounds, 1] = jnp.exp(stat[0, 0] - stat[rounds, 0]) / stat[rounds, 1]

    def widen(g, carry):
        rows = pl.ds(pl.multiple_of(g * block, block), block)
        row = jnp.broadcast_to(stat[rounds, 1, pl.ds(g, 1), :], (block, LANES))
        factor = jnp.sum(jnp.where(diagonal, row, 0.0), axis=1, keepdims=True)
        factor = jnp.broadcast_to(factor, (block, LANES))
        valid = valid_ref[pl.ds(pl.multiple_of(g * block, block) + rim, block), :] > 0
        f_ref[rows, :] = jnp.where(valid, factor, -1.0)
        return carry

    lax.fori_loop(0, ext // block, widen, 0)

    def map_gradient(c):
        first = (lane + c * chunk).astype(jnp.float32)

        def body(g, carry):
            for i in range(GROUPS):
                rows = pl.ds(pl.multiple_of(g * block + 8 * i, 8), 8)
                hit = jnp.where(lab_ref[rows, :] == first, 1.0, 0.0)
                factor = f_ref[rows, :]
                value = e_ref[c, rows, :] * jnp.maximum(factor, 0.0) - hit
                grad[rows, :] = jnp.where(factor >= 0.0, value, 0.0)
            return carry

        lax.fori_loop(0, ext // block, body, 0)

    def score_gradient(c):
        taps = spread_taps(kern_ref, at(c))

        def body(g, carry):
            base = pl.multiple_of(g * block, block)
            sums = tap_block(lambda o: grad[pl.ds(base + o, 8), :], taps, True)
            valid = f_ref[pl.ds(base + rim, block), :] >= 0.0
            total = jnp.where(valid, jnp.concatenate(sums, axis=0), 0.0)
            sg_ref[pl.ds(base, block), at(c)] = total.astype(jnp.bfloat16)
            return carry

        lax.fori_loop(0, row_count // block, body, 0)

    def tap_gradient(c):
        def body(g, sums):
            base = pl.multiple_of(g * block, block)
            held = [grad[pl.ds(base + rim + 8 * i, 8), :] for i in range(GROUPS)]
            sums = list(sums)
            for o in range(8 * (GROUPS - 1) + taps_n):
                v = sc_ref[c, pl.ds(base + rim + o, 8), :]
                for i in range(GROUPS):
                    j = o - 8 * i
                    if 0 <= j < taps_n:
                        sums[j] = sums[j] + held[i] * v
            return tuple(sums)

        zero = jnp.zeros((8, LANES), jnp.float32)
        sums = lax.fori_loop(0, row_count // block, body, (zero,) * taps_n)
        for j in range(taps_n):
            ksum[j : j + 1, :] = jnp.sum(sums[j], axis=0, keepdims=True)

    def start(c):
        map_gradient(c)
        score_gradient(c)
        tap_gradient(c)
        part = lax.dot_general(
            sg_ref[:, at(c)],
            fr_ref[...],
            (((0,), (0,)), ((), ())),
            preferred_element_type=jnp.float32,
        )
        for p in range(recs):
            j = bit_reversed(p, bits)
            acc[0][p, at(c), :] = part[:, j * cols : (j + 1) * cols]
        kacc[0][c] = ksum[...]
        for one in rec_copies(0, c):
            one.start()

    def exchange(k, c):
        total, ktotal = summed(k - 1, c)
        acc[k][:, at(c), :] = total
        kacc[k][c] = ktotal
        for one in rec_copies(k, c):
            one.start()

    def gather_in(c):
        total, ktotal = summed(bits - 1, c)
        mid[at(c), :] = total[0]
        kmid[c] = ktotal

        @pl.when(jnp.logical_not(is_end))
        def _():
            for one in inward_copies(c, False):
                one.wait_recv()
            mid[at(c), :] += outer[at(c), :]
            kmid[c] += kouter[c]

        @pl.when(is_mid)
        def _():
            for one in inward_copies(c, True):
                one.start()

        @pl.when(jnp.logical_not(is_mid))
        def _():
            for one in inward_copies(c, False):
                one.start()

    def spread_out(c):
        for one in inward_copies(c, True):
            one.wait_recv()

        @pl.when(is_mid)
        def _():
            inner[at(c), :] += mid[at(c), :]
            kinner[c] += kmid[c]

        @pl.when(jnp.logical_not(is_end))
        def _():
            for one in outward_copies(c):
                one.start()

        gq_ref[at(c), :] = (inner[at(c), :] * scale).astype(gq_ref.dtype)
        gk_ref[:, at(c)] = kinner[c]

    def send_frames():
        for d in range(1, peers):
            f_compute(lax.rem(y + d, peers))
            f_copy(d).start()

    reach = half - 1
    away = jnp.where(low, reach - t, t - half)
    in_lag = bits + 1 + 2 * (reach - away)
    out_lag = bits + 3 + 2 * (reach + away)
    last_lag = bits + 3 + 4 * reach
    stages = [(0, start), (out_lag, spread_out), (in_lag, gather_in)]
    stages += [(k, functools.partial(exchange, k)) for k in range(bits - 1, 0, -1)]

    def step(s, carry):
        for delay, stage in stages:
            @pl.when((s >= delay) & (s < count + delay))
            def _(stage=stage, delay=delay):
                stage(s - delay)

        @pl.when(s == count - 1)
        def _():
            send_frames()

        @pl.when(s == count + 1)
        def _():
            f_compute(y)

        return carry

    lax.fori_loop(0, count + last_lag, step, 0)

    for d in range(1, peers):
        f_copy(d).wait_recv()
    total = fpart[y]
    for d in range(1, peers):
        total = total + fin[d - 1]
    gf_ref[...] = (total * scale).astype(gf_ref.dtype)
    for d in range(1, peers):
        f_copy(d).wait_send()

    def drain(c, carry):
        for k in range(bits):
            for one in rec_copies(k, c):
                one.wait_send()
        for one in inward_copies(c, False):
            one.wait_send()

        @pl.when(jnp.logical_not(is_end))
        def _():
            for one in outward_copies(c):
                one.wait_send()

        return carry

    lax.fori_loop(0, count, drain, 0)
    for k in range(rounds):
        stat_copy(k).wait_send()
    for side in range(2):
        @pl.when(has[side])
        def _(side=side):
            halo_copy(side).wait_send()


def gradients(labels, lengths, frame_rows, queries, kernel, scale):
    tms, peers, recs = (lax.axis_size("tm"), lax.axis_size("query"), lax.axis_size("rec"))
    bits = recs.bit_length() - 1
    row_count, width = frame_rows.shape
    query_count = queries.shape[0]
    taps = kernel.shape[0]
    chunk = LANES
    count = query_count // chunk
    cols, fcols = (width // recs, width // peers)
    rim = taps // 2
    ext, wide = (row_count + 2 * rim, row_count + 4 * rim)
    rounds = peers.bit_length() - 1
    stat_rows = (ext // (8 * GROUPS) + 7) // 8 * 8
    f32 = jnp.float32
    small = pltpu.VMEM((count, taps, chunk), f32)
    block = pltpu.VMEM((query_count, cols), f32)
    scratch = [pltpu.VMEM((recs >> k, query_count, cols), f32) for k in range(bits)]
    scratch += [pltpu.VMEM((recs >> (k + 1), query_count, cols), f32) for k in range(bits)]
    scratch += [small] * (2 * bits) + [block] * 3 + [small] * 3
    scratch += [
        pltpu.VMEM((peers, row_count, fcols), f32),
        pltpu.VMEM((peers - 1, row_count, fcols), f32),
        pltpu.VMEM((row_count, query_count), jnp.bfloat16),
        pltpu.VMEM((ext, chunk), f32),
        pltpu.VMEM((taps, chunk), f32),
        pltpu.VMEM((count, wide, chunk), f32),
        pltpu.VMEM((count, ext, chunk), f32),
        pltpu.VMEM((ext, chunk), f32),
        pltpu.VMEM((ext, chunk), f32),
        pltpu.VMEM((wide, chunk), f32),
        pltpu.VMEM((wide, width), jnp.bfloat16),
        pltpu.VMEM((2, 2 * rim, width + LANES), f32),
        pltpu.VMEM((2, 2 * rim, width + LANES), f32),
        pltpu.VMEM((rounds + 1, 2, stat_rows, LANES), f32),
        pltpu.VMEM((rounds, 2, stat_rows, LANES), f32),
    ]
    dma = pltpu.SemaphoreType.DMA
    scratch += [dma((bits, 2, count))] * 2 + [dma((2, count))] * 4 + [dma((peers - 1,))] * 2
    scratch += [dma((2,))] * 2 + [dma((rounds,))] * 2
    vmem = pl.BlockSpec(memory_space=pltpu.VMEM)
    return pl.pallas_call(
        functools.partial(gradient_kernel, (tms, peers, recs, chunk), scale),
        out_shape=(
            jax.ShapeDtypeStruct((row_count, fcols), jnp.bfloat16),
            jax.ShapeDtypeStruct((query_count, cols), jnp.bfloat16),
            jax.ShapeDtypeStruct((taps, query_count), f32),
        ),
        in_specs=[vmem, pl.BlockSpec(memory_space=pltpu.SMEM), vmem, vmem, vmem],
        out_specs=(vmem,) * 3,
        scratch_shapes=scratch,
        compiler_params=pltpu.CompilerParams(
            collective_id=0, has_side_effects=True, vmem_limit_bytes=60 * 1024 * 1024
        ),
        name="gradients",
    )(labels, lengths, frame_rows, queries, kernel)


def per_device(frames, queries, kernel, labels, lengths):
    frame_rows = frames[0]
    row_count, width = frame_rows.shape
    logit_scale = 10.0 / math.sqrt(width)
    label_wide = jnp.broadcast_to(labels[0][:, None], (row_count, LANES))
    grad_frames, grad_queries, grad_kernel = gradients(
        label_wide, lengths, frame_rows, queries, kernel, logit_scale
    )
    return (grad_frames[None], grad_queries, grad_kernel)


def solution(mesh):
    in_specs = (P("rec", "tm", None), P("query", None), P(None, "query"), P("rec", "tm"), P("rec"))
    out_specs = (P("rec", "tm", "query"), P("query", "rec"), P(None, "query"))
    return jax.shard_map(
        per_device, mesh=mesh, in_specs=in_specs, out_specs=out_specs, check_vma=False
    )
```

profile of v0, /device:TPU:0, one launch (start us, length us, event | category | flops | bytes accessed | tf_op | source)
XLA Modules:
  0.0 122.2 jit_solution(12281221673126075320)
XLA Ops:
  1.3 1.5 %broadcast_in_dim.11.own_lab_ref = s32[512,128]{1,0:T(8,128)} broadcast(s32[512]{0:T(512)} %bitcast.5), dimensions={0} | broadcast | bytes 264192 | tf_op jit(solution)/shard_map/broadcast_in_dim | solution.py:534
  2.8 113.5 %gradients.1 = (bf16[512,512]{1,0:T(8,128)(2,1)}, bf16[2048,256]{1,0:T(8,128)(2,1)}, f32[33,2048]{1,0:T(8,128)}) custom-call(s32[512,128]{1,0:T(8,128)} %broadcast_in_dim.11.own_lab_ref, s32[1]{0:T(128)S(6)} %copy.11.len_ref, bf16[512,1024]{1,0:T(8,128)(2,1)} %bitcast.3, bf16[2048,1024]{1,0:T(8,128)(2,1)} %qu_ref.1, f32[33,2048]{1,0:T(8,128)} %kern_ref.1), custom_call_target="tpu_custom_call" | custom-call | tf_op jit(solution)/shard_map/gradients/pallas_call | solution.py:513
  116.3 1.9 %copy.12 = bf16[1,512,512]{2,1,0:T(8,128)(2,1)} copy(bf16[1,512,512]{2,1,0:T(8,128)(2,1)} %bitcast.4) | data formatting | bytes 1048576
  118.2 2.3 %copy.13 = bf16[2048,256]{1,0:T(8,128)(2,1)} copy(bf16[2048,256]{1,0:T(8,128)(2,1)} %get-tuple-element.13) | data formatting | bytes 2097152
  120.5 1.7 %copy.14 = f32[33,2048]{1,0:T(8,128)} copy(f32[33,2048]{1,0:T(8,128)} %get-tuple-element.14) | data formatting | bytes 540672
where the time goes:
time: 122 us
  Pallas kernels  114 us (93%)
  local copies, waits for them, and re-layouts  7.37 us (6%)
  between operations  1.29 us (1%)
    pallas_call x1, Pallas kernels, gradients(): pl.pallas_call(functools.partial(gradient_kernel, (tms, peers, recs, chun...  114 us
    unnamed x3, local copies, waits for them, and re-layouts  5.85 us

commit v1 on v0

v1 whole, which is shorter than its diff:
```python
import functools
import math

import jax
import jax.numpy as jnp
from jax import lax
from jax.experimental import pallas as pl
from jax.experimental.pallas import tpu as pltpu
from jax.sharding import PartitionSpec as P


GROUPS = 4
LANES = 128


def spread_taps(kern_ref, lanes):
    taps = kern_ref.shape[0]
    return [jnp.broadcast_to(kern_ref[j : j + 1, lanes], (8, LANES)) for j in range(taps)]


def tap_block(load, taps, flipped):
    count = len(taps)
    sums = [None] * GROUPS
    for o in range(8 * (GROUPS - 1) + count):
        v = load(o)
        for i in range(GROUPS):
            j = o - 8 * i
            if 0 <= j < count:
                term = taps[count - 1 - j if flipped else j] * v
                sums[i] = term if sums[i] is None else sums[i] + term
    return sums


MESH = pl.DeviceIdType.MESH


def bit_reversed(p, bits):
    return sum(((p >> k) & 1) << (bits - 1 - k) for k in range(bits))


def gradient_kernel(dims, scale, lab_hbm, len_hbm, fr_hbm, qu_hbm, kern_hbm, *refs):
    tms, peers, recs, chunk, sub, hop, tap_hop = dims
    bits = recs.bit_length() - 1
    gf_ref, gq_ref, gk_ref = refs[:3]
    scratch = refs[3:]
    acc, scratch = scratch[:bits], scratch[bits:]
    arrived, scratch = scratch[:bits], scratch[bits:]
    kacc, ksum, karrived, scratch = (scratch[0], scratch[1], scratch[2], scratch[3:])
    (mid, outer, inner, kmid, kouter, kinner, kgot, fpart, fin, sg_ref, grad) = scratch[:11]
    (sc_ref, e_ref, f_ref, lab_ref, valid_ref, xh_ref, hin, hout, stat, stat_in) = scratch[11:21]
    (fr_ref, qu_ref, kern_ref, lab_row, lab_in, len_ref) = scratch[21:27]
    scratch = scratch[27:]
    (rec_send, rec_recv, in_send, out_recv, out_send, inn_recv, f_send, f_recv) = scratch[:8]
    (h_send, h_recv, s_send, s_recv, load_sem, qu_sem) = scratch[8:14]
    (k_send, k_recv, kin_send, kout_recv, kout_send, kinn_recv, kg_send, kg_recv) = scratch[14:]

    t = lax.axis_index("tm")
    y = lax.axis_index("query")
    r = lax.axis_index("rec")
    half = tms // 2
    low = t < half
    is_end = (t == 0) | (t == tms - 1)
    is_mid = (t == half - 1) | (t == half)
    inward = jnp.where(low, t + 1, t - 1)
    outward = jnp.where(low, lax.rem(t + tms - 1, tms), lax.rem(t + 1, tms))
    my_bits = [lax.rem(r // (1 << k), 2) for k in range(bits)]
    rec_peers = [r + (1 - 2 * my_bits[k]) * (1 << k) for k in range(bits)]

    barrier = pltpu.get_barrier_semaphore()

    def greet(device):
        pl.semaphore_signal(barrier, inc=1, device_id=device, device_id_type=MESH)

    for peer in rec_peers:
        greet({"rec": peer})
    for d in range(1, peers):
        greet({"query": lax.rem(y + d, peers)})
    greet({"tm": inward})

    @pl.when(jnp.logical_not(is_end))
    def _():
        greet({"tm": outward})

    loads = [
        pltpu.make_async_copy(src, dst, load_sem.at[i])
        for i, (src, dst) in enumerate(
            ((fr_hbm, fr_ref), (lab_hbm, lab_row), (len_hbm, len_ref), (kern_hbm, kern_ref))
        )
    ]
    queries, width = qu_ref.shape
    parts = qu_sem.shape[0]
    span = queries // parts

    def qu_load(p):
        rows = pl.ds(p * span, span)
        return pltpu.make_async_copy(qu_hbm.at[rows], qu_ref.at[rows], qu_sem.at[p])

    for one in loads[:3]:
        one.start()
    for p in range(parts):
        qu_load(p).start()
    loads[3].start()

    count = queries // chunk
    subs = queries // sub
    per = chunk // sub
    rate = per // 2
    cols = width // recs
    fcols = width // peers
    row_count = sg_ref.shape[0]
    taps_n = kern_ref.shape[0]
    rim = taps_n // 2
    halo = 2 * rim
    block = 8 * GROUPS
    ext = f_ref.shape[0]
    tiles = e_ref.shape[0]
    wide = valid_ref.shape[0]
    lane = lax.broadcasted_iota(jnp.int32, (8, LANES), 1) + y * queries

    def copy(src, dst, send, recv, device):
        return pltpu.make_async_remote_copy(
            src_ref=src,
            dst_ref=dst,
            send_sem=send,
            recv_sem=recv,
            device_id=device,
            device_id_type=MESH,
        )

    def at(c):
        return pl.ds(pl.multiple_of(c * chunk, chunk), chunk)

    def sub_at(j):
        return pl.ds(pl.multiple_of(j * sub, sub), sub)

    def f_copy(d):
        p = lax.rem(y + d, peers)
        return copy(fpart.at[p], fin.at[d - 1], f_send.at[d - 1], f_recv.at[d - 1], {"query": p})

    def f_compute(p):
        tile = 128
        columns = pl.ds(pl.multiple_of(p * fcols, fcols), fcols)

        def body(i, carry):
            rows = pl.ds(pl.multiple_of(i * tile, tile), tile)
            fpart[p, rows, :] = jnp.dot(
                sg_ref[rows, :], qu_ref[:, columns], preferred_element_type=jnp.float32
            )
            return carry

        lax.fori_loop(0, row_count // tile, body, 0)

    has = [t > 0, t < tms - 1]

    def halo_copies(side):
        device = {"tm": lax.rem(t + (tms - 1 if side == 0 else 1), tms)}
        return (
            copy(
                hout.at[side],
                hin.at[1 - side],
                h_send.at[0, side],
                h_recv.at[0, 1 - side],
                device,
            ),
            copy(
                lab_row,
                lab_in.at[1 - side],
                h_send.at[1, side],
                h_recv.at[1, 1 - side],
                device,
            ),
        )

    loads[0].wait()
    for side, begin in enumerate((0, row_count - halo)):
        hout[side] = fr_ref[begin : begin + halo, :].astype(jnp.float32)
    loads[1].wait()
    pl.semaphore_wait(barrier, jnp.where(is_end, bits + peers, bits + peers + 1))

    for side in range(2):
        @pl.when(has[side])
        def _(side=side):
            for one in halo_copies(side):
                one.start()

    loads[2].wait()
    frame = lax.broadcasted_iota(jnp.int32, (wide, LANES), 0) + (t * row_count - halo)
    valid_ref[...] = jnp.where((frame >= 0) & (frame < len_ref[0]), 1.0, 0.0)
    stat[...] = jnp.zeros_like(stat)
    f_ref[...] = jnp.full_like(f_ref, -jnp.inf)

    def column_of(row):
        return jnp.transpose(jnp.broadcast_to(row.astype(jnp.float32), (LANES, LANES)))

    for i in range(row_count // LANES):
        lab_ref[rim + i * LANES : rim + (i + 1) * LANES, :] = column_of(
            lab_row[:, i * LANES : (i + 1) * LANES]
        )

    def store_scores(c, rows, part):
        for h in range(2):
            one = part[:, h * LANES : (h + 1) * LANES] * scale
            sc_ref[2 * c + h, rows, :] = jnp.where(valid_ref[rows, :] > 0, one, 0.0)

    def score(c, carry):
        rows = pl.ds(pl.multiple_of(c * 2 * LANES, 2 * LANES), 2 * LANES)
        part = lax.dot_general(
            fr_ref[...],
            qu_ref[rows, :],
            (((1,), (1,)), ((), ())),
            preferred_element_type=jnp.float32,
        )
        store_scores(c, slice(halo, halo + row_count), part)
        return carry

    each = tiles // 2 // parts
    for p in range(parts):
        qu_load(p).wait()
        lax.fori_loop(p * each, (p + 1) * each, score, 0)

    for side in range(2):
        @pl.when(has[side])
        def _(side=side):
            for one in halo_copies(1 - side):
                one.wait_recv()

        @pl.when(jnp.logical_not(has[side]))
        def _(side=side):
            hin[side] = jnp.zeros((halo, width), jnp.float32)
            lab_in[side] = jnp.zeros((1, row_count), jnp.int32)

    xh_ref[:halo, :] = hin[0].astype(jnp.bfloat16)
    xh_ref[halo:, :] = hin[1].astype(jnp.bfloat16)
    lab_ref[:rim, :] = column_of(lab_in[0, :, row_count - LANES :])[LANES - rim :, :]
    lab_ref[rim + row_count :, :] = column_of(lab_in[1, :, :LANES])[:rim, :]

    def halo_score(c, carry):
        rows = pl.ds(pl.multiple_of(c * 2 * LANES, 2 * LANES), 2 * LANES)
        part = lax.dot_general(
            xh_ref[...],
            qu_ref[rows, :],
            (((1,), (1,)), ((), ())),
            preferred_element_type=jnp.float32,
        )
        store_scores(c, slice(0, halo), part[:halo])
        store_scores(c, slice(halo + row_count, wide), part[halo:])
        return carry

    lax.fori_loop(0, tiles // 2, halo_score, 0)
    loads[3].wait()

    def smoothed(c, carry):
        taps = spread_taps(kern_ref, at(c))

        def body(g, carry):
            base = pl.multiple_of(g * block, block)
            sums = tap_block(lambda o: sc_ref[c, pl.ds(base + o, 8), :], taps, False)
            for i in range(GROUPS):
                rows = pl.ds(base + 8 * i, 8)
                e_ref[c, rows, :] = sums[i]
                f_ref[rows, :] = jnp.maximum(f_ref[rows, :], sums[i])
            return carry

        return lax.fori_loop(0, ext // block, body, carry)

    lax.fori_loop(0, tiles, smoothed, 0)

    diagonal = lax.broadcasted_iota(jnp.int32, (block, LANES), 0) == lax.broadcasted_iota(
        jnp.int32, (block, LANES), 1
    )

    def finish(g, carry):
        rows = pl.ds(pl.multiple_of(g * block, block), block)
        top = jnp.max(f_ref[rows, :], axis=1, keepdims=True)
        top = jnp.broadcast_to(top, (block, LANES))
        total = jnp.zeros((block, LANES), jnp.float32)
        for c in range(tiles):
            e = jnp.exp(e_ref[c, rows, :] - top)
            e_ref[c, rows, :] = e
            total = total + e
        total = jnp.broadcast_to(jnp.sum(total, axis=1, keepdims=True), (block, LANES))
        for i, value in enumerate((top, total)):
            picked = jnp.where(diagonal, value, 0.0)
            stat[0, i, pl.ds(g, 1), :] = jnp.sum(picked, axis=0, keepdims=True)
        return carry

    lax.fori_loop(0, ext // block, finish, 0)

    def stat_copy(k):
        bit = lax.rem(y // (1 << k), 2)
        device = {"query": y + (1 - 2 * bit) * (1 << k)}
        return copy(stat.at[k], stat_in.at[k], s_send.at[k], s_recv.at[k], device)

    rounds = peers.bit_length() - 1
    for k in range(rounds):
        stat_copy(k).start()
        stat_copy(k).wait_recv()
        top = jnp.maximum(stat[k, 0], stat_in[k, 0])
        stat[k + 1, 0] = top
        stat[k + 1, 1] = stat[k, 1] * jnp.exp(stat[k, 0] - top) + stat_in[k, 1] * jnp.exp(
            stat_in[k, 0] - top
        )
    stat[rounds, 1] = jnp.exp(stat[0, 0] - stat[rounds, 0]) / stat[rounds, 1]

    def widen(g, carry):
        rows = pl.ds(pl.multiple_of(g * block, block), block)
        row = jnp.broadcast_to(stat[rounds, 1, pl.ds(g, 1), :], (block, LANES))
        factor = jnp.sum(jnp.where(diagonal, row, 0.0), axis=1, keepdims=True)
        factor = jnp.broadcast_to(factor, (block, LANES))
        valid = valid_ref[pl.ds(pl.multiple_of(g * block, block) + rim, block), :] > 0
        f_ref[rows, :] = jnp.where(valid, factor, -1.0)
        return carry

    lax.fori_loop(0, ext // block, widen, 0)

    def map_gradient(c):
        first = (lane + c * chunk).astype(jnp.float32)

        def body(g, carry):
            for i in range(GROUPS):
                rows = pl.ds(pl.multiple_of(g * block + 8 * i, 8), 8)
                hit = jnp.where(lab_ref[rows, :] == first, 1.0, 0.0)
                factor = f_ref[rows, :]
                value = e_ref[c, rows, :] * jnp.maximum(factor, 0.0) - hit
                grad[c, rows, :] = jnp.where(factor >= 0.0, value, 0.0)
            return carry

        lax.fori_loop(0, ext // block, body, 0)

    def score_gradient(c):
        taps = spread_taps(kern_ref, at(c))

        def body(g, carry):
            base = pl.multiple_of(g * block, block)
            sums = tap_block(lambda o: grad[c, pl.ds(base + o, 8), :], taps, True)
            valid = f_ref[pl.ds(base + rim, block), :] >= 0.0
            total = jnp.where(valid, jnp.concatenate(sums, axis=0), 0.0)
            sg_ref[pl.ds(base, block), at(c)] = total.astype(jnp.bfloat16)
            return carry

        lax.fori_loop(0, row_count // block, body, 0)

    def tap_gradient(c):
        def body(g, sums):
            base = pl.multiple_of(g * block, block)
            held = [grad[c, pl.ds(base + rim + 8 * i, 8), :] for i in range(GROUPS)]
            sums = list(sums)
            for o in range(8 * (GROUPS - 1) + taps_n):
                v = sc_ref[c, pl.ds(base + rim + o, 8), :]
                for i in range(GROUPS):
                    j = o - 8 * i
                    if 0 <= j < taps_n:
                        sums[j] = sums[j] + held[i] * v
            return tuple(sums)

        zero = jnp.zeros((8, LANES), jnp.float32)
        sums = lax.fori_loop(0, row_count // block, body, (zero,) * taps_n)
        for j in range(taps_n):
            kacc[c, j : j + 1, :] = jnp.sum(sums[j], axis=0, keepdims=True)

    def rec_copy(k, j):
        n = recs >> k
        theirs = (1 - my_bits[k]) * (n // 2)
        return copy(
            acc[k].at[pl.ds(theirs, n // 2), sub_at(j)],
            arrived[k].at[:, sub_at(j)],
            rec_send.at[k, j],
            rec_recv.at[k, j],
            {"rec": rec_peers[k]},
        )

    def summed(k, j):
        rec_copy(k, j).wait_recv()
        n = recs >> k
        mine = my_bits[k] * (n // 2)
        return acc[k][pl.ds(mine, n // 2), sub_at(j), :] + arrived[k][:, sub_at(j), :]

    def inward_copy(j, to_mid):
        big = inner if to_mid else outer
        recv = inn_recv if to_mid else out_recv
        return copy(mid.at[sub_at(j)], big.at[sub_at(j)], in_send.at[j], recv.at[j], {"tm": inward})

    def outward_copy(j):
        return copy(
            inner.at[sub_at(j)],
            inner.at[sub_at(j)],
            out_send.at[j],
            inn_recv.at[j],
            {"tm": outward},
        )

    def produce(c):
        map_gradient(c)
        score_gradient(c)
        part = lax.dot_general(
            sg_ref[:, at(c)],
            fr_ref[...],
            (((0,), (0,)), ((), ())),
            preferred_element_type=jnp.float32,
        )
        for p in range(recs):
            j = bit_reversed(p, bits)
            acc[0][p, at(c), :] = part[:, j * cols : (j + 1) * cols]
        for h in range(per):
            rec_copy(0, c * per + h).start()

    def exchange(k, j):
        acc[k][:, sub_at(j), :] = summed(k - 1, j)
        rec_copy(k, j).start()

    def gather_in(j):
        mid[sub_at(j), :] = summed(bits - 1, j)[0]

        @pl.when(jnp.logical_not(is_end))
        def _():
            inward_copy(j, False).wait_recv()
            mid[sub_at(j), :] += outer[sub_at(j), :]

        @pl.when(is_mid)
        def _():
            inward_copy(j, True).start()

        @pl.when(jnp.logical_not(is_mid))
        def _():
            inward_copy(j, False).start()

    def spread_out(j):
        inward_copy(j, True).wait_recv()

        @pl.when(is_mid)
        def _():
            inner[sub_at(j), :] += mid[sub_at(j), :]

        @pl.when(jnp.logical_not(is_end))
        def _():
            outward_copy(j).start()

        gq_ref[sub_at(j), :] = (inner[sub_at(j), :] * scale).astype(gq_ref.dtype)
        for k in range(bits):
            rec_copy(k, j).wait_send()
        inward_copy(j, False).wait_send()

    def k_copy(k, i):
        src = kacc.at[2 * i + 1 - my_bits[0]] if k == 0 else ksum.at[k - 1, i]
        return copy(src, karrived.at[k, i], k_send.at[k, i], k_recv.at[k, i], {"rec": rec_peers[k]})

    def k_summed(k, i):
        k_copy(k, i).wait_recv()
        own = kacc[2 * i + my_bits[0]] if k == 0 else ksum[k - 1, i]
        return own + karrived[k, i]

    def k_inward(i, to_mid):
        dst = kinner if to_mid else kouter
        recv = kinn_recv if to_mid else kout_recv
        return copy(kmid.at[i], dst.at[i], kin_send.at[i], recv.at[i], {"tm": inward})

    def k_outward(i):
        return copy(kinner.at[i], kinner.at[i], kout_send.at[i], kinn_recv.at[i], {"tm": outward})

    def k_give(i):
        return copy(kinner.at[i], kgot.at[i], kg_send.at[i], kg_recv.at[i], {"rec": rec_peers[0]})

    def k_exchange(k, i):
        ksum[k - 1, i] = k_summed(k - 1, i)
        k_copy(k, i).start()

    def k_gather(i):
        kmid[i] = k_summed(bits - 1, i)

        @pl.when(jnp.logical_not(is_end))
        def _():
            k_inward(i, False).wait_recv()
            kmid[i] += kouter[i]

        @pl.when(is_mid)
        def _():
            k_inward(i, True).start()

        @pl.when(jnp.logical_not(is_mid))
        def _():
            k_inward(i, False).start()

    def k_spread(i):
        k_inward(i, True).wait_recv()

        @pl.when(is_mid)
        def _():
            kinner[i] += kmid[i]

        k_give(i).start()

        @pl.when(jnp.logical_not(is_end))
        def _():
            k_outward(i).start()

        gk_ref[:, at(2 * i + my_bits[0])] = kinner[i]
        for k in range(bits):
            k_copy(k, i).wait_send()
        k_inward(i, False).wait_send()

    def k_take(i):
        k_give(i).wait_recv()
        gk_ref[:, at(2 * i + 1 - my_bits[0])] = kgot[i]

    reach = half - 1
    away = jnp.where(low, reach - t, t - half)

    def plan(step, first, spread, gather, swap, take):
        base = first + (bits - 1) * step
        ends = base + 2 * step * reach + step
        late = [(ends + first, take)] if take else []
        late += [(base + step * (reach + away + 1), spread), (base + step * (reach - away), gather)]
        late += [
            (first + (k - 1) * step, functools.partial(swap, k)) for k in range(bits - 1, 0, -1)
        ]
        return late, ends + (first if take else 0)

    stages, last = plan(hop, rate, spread_out, gather_in, exchange, None)
    k_stages, k_last = plan(tap_hop, 1, k_spread, k_gather, k_exchange, k_take)
    begun = 2 * count
    steps = begun + max((last + rate - 1) // rate, k_last)

    def step(s, carry):
        @pl.when(s < count)
        def _():
            produce(s)

        @pl.when(s == count)
        def _():
            for d in range(1, peers):
                f_compute(lax.rem(y + d, peers))
                f_copy(d).start()

        @pl.when(s == begun)
        def _():
            f_compute(y)

        c = s - count

        @pl.when((c >= 0) & (c < count))
        def _():
            tap_gradient(c)

            @pl.when(lax.rem(c, 2) == 1)
            def _():
                k_copy(0, c // 2).start()

        for i in range(rate):
            for delay, stage in stages:
                tick = s * rate + i - delay

                @pl.when((tick >= 0) & (tick < subs))
                def _(stage=stage, tick=tick):
                    stage(tick)

        for delay, stage in k_stages:
            tick = c - delay

            @pl.when((tick >= 0) & (tick < count) & (lax.rem(tick + 2, 2) == 1))
            def _(stage=stage, tick=tick):
                stage(tick // 2)

        return carry

    lax.fori_loop(0, steps, step, 0)

    for d in range(1, peers):
        f_copy(d).wait_recv()
    total = fpart[y]
    for d in range(1, peers):
        total = total + fin[d - 1]
    gf_ref[...] = (total * scale).astype(gf_ref.dtype)
    for d in range(1, peers):
        f_copy(d).wait_send()

    @pl.when(jnp.logical_not(is_end))
    def _():
        def drain(j, carry):
            outward_copy(j).wait_send()
            return carry

        lax.fori_loop(0, subs, drain, 0)

    def k_drain(i, carry):
        k_give(i).wait_send()

        @pl.when(jnp.logical_not(is_end))
        def _():
            k_outward(i).wait_send()

        return carry

    lax.fori_loop(0, count // 2, k_drain, 0)
    for k in range(rounds):
        stat_copy(k).wait_send()
    for side in range(2):
        @pl.when(has[side])
        def _(side=side):
            for one in halo_copies(side):
                one.wait_send()


SPLIT = 2
HOP = 3
TAP_HOP = 2
PARTS = 2


def gradients(labels, lengths, frame_rows, queries, kernel, scale):
    tms, peers, recs = (lax.axis_size("tm"), lax.axis_size("query"), lax.axis_size("rec"))
    bits = recs.bit_length() - 1
    row_count, width = frame_rows.shape
    query_count = queries.shape[0]
    taps = kernel.shape[0]
    chunk = LANES
    sub = chunk // SPLIT
    count = query_count // chunk
    subs = query_count // sub
    cols, fcols = (width // recs, width // peers)
    rim = taps // 2
    ext, wide = (row_count + 2 * rim, row_count + 4 * rim)
    rounds = peers.bit_length() - 1
    stat_rows = (ext // (8 * GROUPS) + 7) // 8 * 8
    pairs = count // 2
    f32 = jnp.float32
    vmem = pltpu.VMEM
    small = vmem((pairs, taps, chunk), f32)
    block = vmem((query_count, cols), f32)
    scratch = [vmem((recs >> k, query_count, cols), f32) for k in range(bits)]
    scratch += [vmem((recs >> (k + 1), query_count, cols), f32) for k in range(bits)]
    scratch += [
        vmem((count, taps, chunk), f32),
        vmem((max(bits - 1, 1), pairs, taps, chunk), f32),
        vmem((bits, pairs, taps, chunk), f32),
    ]
    scratch += [block] * 3 + [small] * 4
    scratch += [
        vmem((peers, row_count, fcols), f32),
        vmem((peers - 1, row_count, fcols), f32),
        vmem((row_count, query_count), jnp.bfloat16),
        vmem((count, ext, chunk), f32),
        vmem((count, wide, chunk), f32),
        vmem((count, ext, chunk), f32),
        vmem((ext, chunk), f32),
        vmem((ext, chunk), f32),
        vmem((wide, chunk), f32),
        vmem((4 * rim, width), jnp.bfloat16),
        vmem((2, 2 * rim, width), f32),
        vmem((2, 2 * rim, width), f32),
        vmem((rounds + 1, 2, stat_rows, LANES), f32),
        vmem((rounds, 2, stat_rows, LANES), f32),
        vmem((row_count, width), jnp.bfloat16),
        vmem((query_count, width), jnp.bfloat16),
        vmem((taps, query_count), f32),
        vmem((1, row_count), jnp.int32),
        vmem((2, 1, row_count), jnp.int32),
        pltpu.SMEM((1,), jnp.int32),
    ]
    dma = pltpu.SemaphoreType.DMA
    scratch += [dma((bits, subs))] * 2 + [dma((subs,))] * 4 + [dma((peers - 1,))] * 2
    scratch += [dma((2, 2))] * 2 + [dma((rounds,))] * 2 + [dma((4,)), dma((PARTS,))]
    scratch += [dma((bits, pairs))] * 2 + [dma((pairs,))] * 6
    hbm = pl.BlockSpec(memory_space=pl.ANY)
    dims = (tms, peers, recs, chunk, sub, HOP, TAP_HOP)
    return pl.pallas_call(
        functools.partial(gradient_kernel, dims, scale),
        out_shape=(
            pltpu.VMEM((row_count, fcols), jnp.bfloat16),
            pltpu.VMEM((query_count, cols), jnp.bfloat16),
            pltpu.VMEM((taps, query_count), f32),
        ),
        in_specs=[hbm] * 5,
        out_specs=(pl.BlockSpec(memory_space=pltpu.VMEM),) * 3,
        scratch_shapes=scratch,
        compiler_params=pltpu.CompilerParams(
            collective_id=0, has_side_effects=True, vmem_limit_bytes=60 * 1024 * 1024
        ),
        name="gradients",
    )(labels, lengths, frame_rows, queries, kernel)


def store_kernel(*refs):
    ins, outs, sem = refs[:3], refs[3:6], refs[6]
    copies = [pltpu.make_async_copy(a, b, sem.at[i]) for i, (a, b) in enumerate(zip(ins, outs))]
    for one in copies:
        one.start()
    for one in copies:
        one.wait()


def store(arrays):
    return pl.pallas_call(
        store_kernel,
        out_shape=tuple(jax.ShapeDtypeStruct(a.shape, a.dtype) for a in arrays),
        in_specs=[pl.BlockSpec(memory_space=pltpu.VMEM)] * 3,
        out_specs=(pl.BlockSpec(memory_space=pl.ANY),) * 3,
        scratch_shapes=[pltpu.SemaphoreType.DMA((3,))],
        compiler_params=pltpu.CompilerParams(vmem_limit_bytes=4 * 1024 * 1024),
        name="store",
    )(*arrays)


def per_device(frames, queries, kernel, labels, lengths):
    frame_rows = frames[0]
    width = frame_rows.shape[1]
    logit_scale = 10.0 / math.sqrt(width)
    grad_frames, grad_queries, grad_kernel = store(
        gradients(labels, lengths, frame_rows, queries, kernel, logit_scale)
    )
    return (grad_frames[None], grad_queries, grad_kernel)


def solution(mesh):
    in_specs = (P("rec", "tm", None), P("query", None), P(None, "query"), P("rec", "tm"), P("rec"))
    out_specs = (P("rec", "tm", "query"), P("query", "rec"), P(None, "query"))
    return jax.shard_map(
        per_device, mesh=mesh, in_specs=in_specs, out_specs=out_specs, check_vma=False
    )
```

time: 122 us -> 106 us (0.87)
  Pallas kernels: 114 us -> 105 us
  local copies, waits for them, and re-layouts: 7.37 us -> 0 us
    pallas_call x1 -> x2, Pallas kernels: 114 us -> 105 us  [the longest x1 103 us: gradients(): pl.pallas_call(functools.partial(gradient_kernel, dims, scale), out_shape...]
    unnamed x3 -> x0, local copies, waits for them, and re-layouts: 5.85 us -> none
    broadcast_in_dim x1 -> x0, local copies, waits for them, and re-layouts: 1.52 us -> none  [per_device(): label_wide = jnp.broadcast_to(labels[0][:, None], (row_count, LANES))]
where the time goes in v1:
time: 106 us
  Pallas kernels  105 us (99%)
  between operations  1.29 us (1%)
    pallas_call x1, Pallas kernels, gradients(): pl.pallas_call(functools.partial(gradient_kernel, dims, scale), out_shape...  103 us

profile of v1, /device:TPU:0, one launch (start us, length us, event | category | flops | bytes accessed | tf_op | source)
XLA Modules:
  0.0 106.0 jit_solution(2744421537612476976)
XLA Ops:
  1.3 103.4 %gradients.1 = (bf16[512,512]{1,0:T(8,128)(2,1)S(1)}, bf16[2048,256]{1,0:T(8,128)(2,1)S(1)}, f32[33,2048]{1,0:T(8,128)S(1)}) custom-call(s32[1,512]{1,0:T(1,128)} %lab_hbm.1, s32[1]{0:T(128)S(6)} %copy.8.len_hbm, bf16[512,1024]{1,0:T(8,128)(2,1)} %bitcast.2, bf16[2048,1024]{1,0:T(8,128)(2,1)} %qu_hbm.1, f32[33,2048]{1,0:T(8,128)} %kern_hbm.1), custom_call_target="tpu_custom_call" | custom-call | tf_op jit(solution)/shard_map/gradients/pallas_call | solution.py:665
  104.7 1.3 %store.1 = (bf16[512,512]{1,0:T(8,128)(2,1)}, bf16[2048,256]{1,0:T(8,128)(2,1)}, f32[33,2048]{1,0:T(8,128)}) custom-call(bf16[512,512]{1,0:T(8,128)(2,1)S(1)} %get-tuple-element.9.refs_0_, bf16[2048,256]{1,0:T(8,128)(2,1)S(1)} %get-tuple-element.10.refs_1_, f32[33,2048]{1,0:T(8,128)S(1)} %get-tuple-element.11.refs_2_), custom_call_target="tpu_custom_call" | custom-call | tf_op jit(solution)/shard_map/store/pallas_call | solution.py:692

commit v2 on v1

--- a/solution.py
+++ b/solution.py
@@ -18,17 +18,80 @@
     return [jnp.broadcast_to(kern_ref[j : j + 1, lanes], (8, LANES)) for j in range(taps)]
 
 
-def tap_block(load, taps, flipped):
-    count = len(taps)
-    sums = [None] * GROUPS
-    for o in range(8 * (GROUPS - 1) + count):
-        v = load(o)
-        for i in range(GROUPS):
-            j = o - 8 * i
-            if 0 <= j < count:
-                term = taps[count - 1 - j if flipped else j] * v
-                sums[i] = term if sums[i] is None else sums[i] + term
-    return sums
+SPAN = 4
+AHEAD = 3
+
+
+def plus(a, b):
+    return [x + b[i] if i < len(b) else x for i, x in enumerate(a)]
+
+
+def minus(a):
+    return [-x for x in a]
+
+
+def spread_filters(filt_ref, h):
+    even, odd = h[0::2], h[1::2]
+    both = plus(even, odd)
+    filters = (
+        plus(both[0::2], both[1::2]),
+        both[0::2],
+        minus(both[1::2]),
+        plus(even[0::2], even[1::2]),
+        even[0::2],
+        minus(even[1::2]),
+        minus(plus(odd[0::2], odd[1::2])),
+        minus(odd[0::2]),
+        odd[1::2],
+    )
+    depth = len(filters[0])
+    for n, one in enumerate(filters):
+        for i, x in enumerate(one):
+            filt_ref[n * depth + i] = x
+    return [len(one) for one in filters]
+
+
+def spread_streams(load, strm_ref, groups):
+    def one_group(g):
+        x = [load(pl.multiple_of(g * 32, 32) + o) for o in range(7)]
+        e = [x[o] - x[o + 2] for o in range(5)]
+        f = [e[o] - e[o + 1] for o in range(4)]
+        rows = pl.ds(pl.multiple_of(g * 8, 8), 8)
+        streams = (x[3], e[1], e[3], x[2] - x[3], f[0], f[2], x[3] - x[4], f[1], f[3])
+        for n, one in enumerate(streams):
+            strm_ref[n, rows, :] = one
+
+    def body(i, carry):
+        for k in range(AHEAD):
+            one_group(i * AHEAD + k)
+        return carry
+
+    lax.fori_loop(0, groups // AHEAD, body, 0)
+    for g in range(groups // AHEAD * AHEAD, groups):
+        one_group(g)
+
+
+def fir(strm_ref, filt_ref, lengths, base, span):
+    depth = lengths[0]
+    done = []
+    for n, count in enumerate(lengths):
+        taps = [filt_ref[n * depth + i] for i in range(count)]
+        sums = list(done[n // 3 * 3]) if n % 3 else [None] * span
+        for o in range(8 * (span - 1) + count):
+            v = strm_ref[n, pl.ds(base + o, 8), :]
+            for k in range(span):
+                i = o - 8 * k
+                if 0 <= i < count:
+                    term = taps[i] * v
+                    sums[k] = term if sums[k] is None else sums[k] + term
+        done.append(sums)
+    add = lambda a, b: [x + z for x, z in zip(a, b)]
+    return (
+        add(done[1], done[4]),
+        add(done[1], done[7]),
+        add(done[2], done[5]),
+        add(done[2], done[8]),
+    )
 
 
 MESH = pl.DeviceIdType.MESH
@@ -48,8 +111,8 @@
     kacc, ksum, karrived, scratch = (scratch[0], scratch[1], scratch[2], scratch[3:])
     (mid, outer, inner, kmid, kouter, kinner, kgot, fpart, fin, sg_ref, grad) = scratch[:11]
     (sc_ref, e_ref, f_ref, lab_ref, valid_ref, xh_ref, hin, hout, stat, stat_in) = scratch[11:21]
-    (fr_ref, qu_ref, kern_ref, lab_row, lab_in, len_ref) = scratch[21:27]
-    scratch = scratch[27:]
+    (fr_ref, qu_ref, kern_ref, lab_row, lab_in, len_ref, strm_ref, filt_ref, turn) = scratch[21:30]
+    scratch = scratch[30:]
     (rec_send, rec_recv, in_send, out_recv, out_send, inn_recv, f_send, f_recv) = scratch[:8]
     (h_send, h_recv, s_send, s_recv, load_sem, qu_sem) = scratch[8:14]
     (k_send, k_recv, kin_send, kout_recv, kout_send, kinn_recv, kg_send, kg_recv) = scratch[14:]
@@ -250,18 +313,25 @@
     loads[3].wait()
 
     def smoothed(c, carry):
-        taps = spread_taps(kern_ref, at(c))
+        lengths = spread_filters(filt_ref, spread_taps(kern_ref, at(c)))
+        spread_streams(lambda o: sc_ref[c, pl.ds(o, 8, stride=4), :], strm_ref, wide // 32)
+
+        def piece(base, span):
+            for p, sums in enumerate(fir(strm_ref, filt_ref, lengths, base, span)):
+                for k in range(span):
+                    rows = pl.ds(4 * base + 32 * k + p, 8, stride=4)
+                    e_ref[c, rows, :] = sums[k]
+                    f_ref[rows, :] = jnp.maximum(f_ref[rows, :], sums[k])
 
         def body(g, carry):
-            base = pl.multiple_of(g * block, block)
-            sums = tap_block(lambda o: sc_ref[c, pl.ds(base + o, 8), :], taps, False)
-            for i in range(GROUPS):
-                rows = pl.ds(base + 8 * i, 8)
-                e_ref[c, rows, :] = sums[i]
-                f_ref[rows, :] = jnp.maximum(f_ref[rows, :], sums[i])
+            piece(pl.multiple_of(g * 8 * SPAN, 8), SPAN)
             return carry
 
-        return lax.fori_loop(0, ext // block, body, carry)
+        whole = ext // (32 * SPAN)
+        lax.fori_loop(0, whole, body, 0)
+        for g in range(whole * SPAN, ext // 32):
+            piece(8 * g, 1)
+        return carry
 
     lax.fori_loop(0, tiles, smoothed, 0)
 
@@ -328,17 +398,20 @@
         lax.fori_loop(0, ext // block, body, 0)
 
     def score_gradient(c):
-        taps = spread_taps(kern_ref, at(c))
+        lengths = spread_filters(filt_ref, spread_taps(kern_ref, at(c))[::-1])
+        spread_streams(lambda o: grad[c, pl.ds(o, 8, stride=4), :], strm_ref, ext // 32)
 
         def body(g, carry):
-            base = pl.multiple_of(g * block, block)
-            sums = tap_block(lambda o: grad[c, pl.ds(base + o, 8), :], taps, True)
-            valid = f_ref[pl.ds(base + rim, block), :] >= 0.0
-            total = jnp.where(valid, jnp.concatenate(sums, axis=0), 0.0)
-            sg_ref[pl.ds(base, block), at(c)] = total.astype(jnp.bfloat16)
+            base = pl.multiple_of(g * 8 * SPAN, 8)
+            for p, sums in enumerate(fir(strm_ref, filt_ref, lengths, base, SPAN)):
+                for k in range(SPAN):
+                    turn[pl.ds(32 * k + p, 8, stride=4), :] = sums[k]
+            rows = pl.ds(pl.multiple_of(g * 32 * SPAN, 32 * SPAN), 32 * SPAN)
+            valid = f_ref[pl.ds(pl.multiple_of(g * 32 * SPAN, 32) + rim, 32 * SPAN), :] >= 0.0
+            sg_ref[rows, at(c)] = jnp.where(valid, turn[...], 0.0).astype(jnp.bfloat16)
             return carry
 
-        lax.fori_loop(0, row_count // block, body, 0)
+        lax.fori_loop(0, row_count // (32 * SPAN), body, 0)
 
     def tap_gradient(c):
         def body(g, sums):
@@ -602,7 +675,7 @@
 
 SPLIT = 2
 HOP = 3
-TAP_HOP = 2
+TAP_HOP = 3
 PARTS = 2
 
 
@@ -638,8 +711,8 @@
         vmem((peers, row_count, fcols), f32),
         vmem((peers - 1, row_count, fcols), f32),
         vmem((row_count, query_count), jnp.bfloat16),
-        vmem((count, ext, chunk), f32),
-        vmem((count, wide, chunk), f32),
+        vmem((count, ext + 8, chunk), f32),
+        vmem((count, wide + 8, chunk), f32),
         vmem((count, ext, chunk), f32),
         vmem((ext, chunk), f32),
         vmem((ext, chunk), f32),
@@ -655,6 +728,9 @@
         vmem((1, row_count), jnp.int32),
         vmem((2, 1, row_count), jnp.int32),
         pltpu.SMEM((1,), jnp.int32),
+        vmem((9, wide // 4, chunk), f32),
+        vmem((9 * (taps // 4 + 1), 8, chunk), f32),
+        vmem((32 * SPAN, chunk), f32),
     ]
     dma = pltpu.SemaphoreType.DMA
     scratch += [dma((bits, subs))] * 2 + [dma((subs,))] * 4 + [dma((peers - 1,))] * 2

time: 106 us -> 101 us (0.953)
  Pallas kernels: 105 us -> 99.8 us
    pallas_call x1, Pallas kernels: 103 us -> 98.5 us  [gradients(): pl.pallas_call(functools.partial(gradient_kernel, dims, scale), out_shape...]
where the time goes in v2:
time: 101 us
  Pallas kernels  99.8 us (99%)
  between operations  1.29 us (1%)
    pallas_call x1, Pallas kernels, gradients(): pl.pallas_call(functools.partial(gradient_kernel, dims, scale), out_shape...  98.5 us

profile of v2, /device:TPU:0, one launch (start us, length us, event | category | flops | bytes accessed | tf_op | source)
XLA Modules:
  0.0 101.1 jit_solution(11628001215514198217)
XLA Ops:
  1.3 98.5 %gradients.1 = (bf16[512,512]{1,0:T(8,128)(2,1)S(1)}, bf16[2048,256]{1,0:T(8,128)(2,1)S(1)}, f32[33,2048]{1,0:T(8,128)S(1)}) custom-call(s32[1,512]{1,0:T(1,128)} %lab_hbm.1, s32[1]{0:T(128)S(6)} %copy.8.len_hbm, bf16[512,1024]{1,0:T(8,128)(2,1)} %bitcast.2, bf16[2048,1024]{1,0:T(8,128)(2,1)} %qu_hbm.1, f32[33,2048]{1,0:T(8,128)} %kern_hbm.1), custom_call_target="tpu_custom_call" | custom-call | tf_op jit(solution)/shard_map/gradients/pallas_call | solution.py:741
  99.8 1.3 %store.1 = (bf16[512,512]{1,0:T(8,128)(2,1)}, bf16[2048,256]{1,0:T(8,128)(2,1)}, f32[33,2048]{1,0:T(8,128)}) custom-call(bf16[512,512]{1,0:T(8,128)(2,1)S(1)} %get-tuple-element.9.refs_0_, bf16[2048,256]{1,0:T(8,128)(2,1)S(1)} %get-tuple-element.10.refs_1_, f32[33,2048]{1,0:T(8,128)S(1)} %get-tuple-element.11.refs_2_), custom_call_target="tpu_custom_call" | custom-call | tf_op jit(solution)/shard_map/store/pallas_call | solution.py:768

commit v3 on v2

--- a/solution.py
+++ b/solution.py
@@ -112,7 +112,7 @@
     (mid, outer, inner, kmid, kouter, kinner, kgot, fpart, fin, sg_ref, grad) = scratch[:11]
     (sc_ref, e_ref, f_ref, lab_ref, valid_ref, xh_ref, hin, hout, stat, stat_in) = scratch[11:21]
     (fr_ref, qu_ref, kern_ref, lab_row, lab_in, len_ref, strm_ref, filt_ref, turn) = scratch[21:30]
-    scratch = scratch[30:]
+    edge_ref, scratch = scratch[30], scratch[31:]
     (rec_send, rec_recv, in_send, out_recv, out_send, inn_recv, f_send, f_recv) = scratch[:8]
     (h_send, h_recv, s_send, s_recv, load_sem, qu_sem) = scratch[8:14]
     (k_send, k_recv, kin_send, kout_recv, kout_send, kinn_recv, kg_send, kg_recv) = scratch[14:]
@@ -144,6 +144,12 @@
     def _():
         greet({"tm": outward})
 
+    edges = [slice(0, 2 * (kern_ref.shape[0] // 2))]
+    edges.append(slice(fr_ref.shape[0] - edges[0].stop, fr_ref.shape[0]))
+    edge_loads = [
+        pltpu.make_async_copy(fr_hbm.at[rows], edge_ref.at[side], load_sem.at[4 + side])
+        for side, rows in enumerate(edges)
+    ]
     loads = [
         pltpu.make_async_copy(src, dst, load_sem.at[i])
         for i, (src, dst) in enumerate(
@@ -158,7 +164,7 @@
         rows = pl.ds(p * span, span)
         return pltpu.make_async_copy(qu_hbm.at[rows], qu_ref.at[rows], qu_sem.at[p])
 
-    for one in loads[:3]:
+    for one in edge_loads + loads[1:3] + loads[:1]:
         one.start()
     for p in range(parts):
         qu_load(p).start()
@@ -171,6 +177,7 @@
     cols = width // recs
     fcols = width // peers
     row_count = sg_ref.shape[0]
+    f_tiles = row_count // LANES
     taps_n = kern_ref.shape[0]
     rim = taps_n // 2
     halo = 2 * rim
@@ -196,22 +203,36 @@
     def sub_at(j):
         return pl.ds(pl.multiple_of(j * sub, sub), sub)
 
-    def f_copy(d):
+    def f_rows(i):
+        return pl.ds(pl.multiple_of(i * LANES, LANES), LANES)
+
+    def f_copy(d, i):
         p = lax.rem(y + d, peers)
-        return copy(fpart.at[p], fin.at[d - 1], f_send.at[d - 1], f_recv.at[d - 1], {"query": p})
-
-    def f_compute(p):
-        tile = 128
+        return copy(
+            fpart.at[p, f_rows(i)],
+            fin.at[d - 1, f_rows(i)],
+            f_send.at[d - 1, i],
+            f_recv.at[d - 1, i],
+            {"query": p},
+        )
+
+    def f_compute(p, i):
         columns = pl.ds(pl.multiple_of(p * fcols, fcols), fcols)
-
-        def body(i, carry):
-            rows = pl.ds(pl.multiple_of(i * tile, tile), tile)
-            fpart[p, rows, :] = jnp.dot(
-                sg_ref[rows, :], qu_ref[:, columns], preferred_element_type=jnp.float32
-            )
-            return carry
-
-        lax.fori_loop(0, row_count // tile, body, 0)
+        fpart[p, f_rows(i), :] = jnp.dot(
+            sg_ref[f_rows(i), :], qu_ref[:, columns], preferred_element_type=jnp.float32
+        )
+
+    def f_finish():
+        for i in range(f_tiles):
+            for d in range(1, peers):
+                f_copy(d, i).wait_recv()
+        total = fpart[y]
+        for d in range(1, peers):
+            total = total + fin[d - 1]
+        gf_ref[...] = (total * scale).astype(gf_ref.dtype)
+        for i in range(f_tiles):
+            for d in range(1, peers):
+                f_copy(d, i).wait_send()
 
     has = [t > 0, t < tms - 1]
 
@@ -234,9 +255,9 @@
             ),
         )
 
-    loads[0].wait()
-    for side, begin in enumerate((0, row_count - halo)):
-        hout[side] = fr_ref[begin : begin + halo, :].astype(jnp.float32)
+    for side in range(2):
+        edge_loads[side].wait()
+        hout[side] = edge_ref[side].astype(jnp.float32)
     loads[1].wait()
     pl.semaphore_wait(barrier, jnp.where(is_end, bits + peers, bits + peers + 1))
 
@@ -250,7 +271,6 @@
     frame = lax.broadcasted_iota(jnp.int32, (wide, LANES), 0) + (t * row_count - halo)
     valid_ref[...] = jnp.where((frame >= 0) & (frame < len_ref[0]), 1.0, 0.0)
     stat[...] = jnp.zeros_like(stat)
-    f_ref[...] = jnp.full_like(f_ref, -jnp.inf)
 
     def column_of(row):
         return jnp.transpose(jnp.broadcast_to(row.astype(jnp.float32), (LANES, LANES)))
@@ -260,26 +280,33 @@
             lab_row[:, i * LANES : (i + 1) * LANES]
         )
 
-    def store_scores(c, rows, part):
-        for h in range(2):
-            one = part[:, h * LANES : (h + 1) * LANES] * scale
-            sc_ref[2 * c + h, rows, :] = jnp.where(valid_ref[rows, :] > 0, one, 0.0)
-
-    def score(c, carry):
-        rows = pl.ds(pl.multiple_of(c * 2 * LANES, 2 * LANES), 2 * LANES)
-        part = lax.dot_general(
-            fr_ref[...],
-            qu_ref[rows, :],
-            (((1,), (1,)), ((), ())),
-            preferred_element_type=jnp.float32,
-        )
-        store_scores(c, slice(halo, halo + row_count), part)
-        return carry
-
-    each = tiles // 2 // parts
+    batch = min(BATCH, tiles // parts)
+
+    def score(rows_of, keep):
+        def body(c, carry):
+            rows = pl.ds(pl.multiple_of(c * batch * LANES, LANES), batch * LANES)
+            part = lax.dot_general(
+                rows_of[...],
+                qu_ref[rows, :],
+                (((1,), (1,)), ((), ())),
+                preferred_element_type=jnp.float32,
+            )
+            for h in range(batch):
+                for begin, rows in keep:
+                    size = rows.stop - rows.start
+                    one = part[begin : begin + size, h * LANES : (h + 1) * LANES] * scale
+                    one = jnp.where(valid_ref[rows, :] > 0, one, 0.0)
+                    sc_ref[batch * c + h, rows, :] = one
+            return carry
+
+        return body
+
+    loads[0].wait()
+    each = tiles // batch // parts
+    own_rows = slice(halo, halo + row_count)
     for p in range(parts):
         qu_load(p).wait()
-        lax.fori_loop(p * each, (p + 1) * each, score, 0)
+        lax.fori_loop(p * each, (p + 1) * each, score(fr_ref, [(0, own_rows)]), 0)
 
     for side in range(2):
         @pl.when(has[side])
@@ -297,19 +324,8 @@
     lab_ref[:rim, :] = column_of(lab_in[0, :, row_count - LANES :])[LANES - rim :, :]
     lab_ref[rim + row_count :, :] = column_of(lab_in[1, :, :LANES])[:rim, :]
 
-    def halo_score(c, carry):
-        rows = pl.ds(pl.multiple_of(c * 2 * LANES, 2 * LANES), 2 * LANES)
-        part = lax.dot_general(
-            xh_ref[...],
-            qu_ref[rows, :],
-            (((1,), (1,)), ((), ())),
-            preferred_element_type=jnp.float32,
-        )
-        store_scores(c, slice(0, halo), part[:halo])
-        store_scores(c, slice(halo + row_count, wide), part[halo:])
-        return carry
-
-    lax.fori_loop(0, tiles // 2, halo_score, 0)
+    outer_rows = [(0, slice(0, halo)), (halo, slice(halo + row_count, wide))]
+    lax.fori_loop(0, tiles // batch, score(xh_ref, outer_rows), 0)
     loads[3].wait()
 
     def smoothed(c, carry):
@@ -321,7 +337,6 @@
                 for k in range(span):
                     rows = pl.ds(4 * base + 32 * k + p, 8, stride=4)
                     e_ref[c, rows, :] = sums[k]
-                    f_ref[rows, :] = jnp.maximum(f_ref[rows, :], sums[k])
 
         def body(g, carry):
             piece(pl.multiple_of(g * 8 * SPAN, 8), SPAN)
@@ -339,22 +354,43 @@
         jnp.int32, (block, LANES), 1
     )
 
-    def finish(g, carry):
+    def widest(g, carry):
         rows = pl.ds(pl.multiple_of(g * block, block), block)
+        top = e_ref[0, rows, :]
+        for c in range(1, tiles):
+            top = jnp.maximum(top, e_ref[c, rows, :])
+        f_ref[rows, :] = top
+        return carry
+
+    lax.fori_loop(0, ext // block, widest, 0)
+
+    def note(i, g, value):
+        picked = jnp.where(diagonal, value, 0.0)
+        stat[0, i, pl.ds(g, 1), :] = jnp.sum(picked, axis=0, keepdims=True)
+
+    for g in range(ext // block):
+        rows = pl.ds(g * block, block)
         top = jnp.max(f_ref[rows, :], axis=1, keepdims=True)
         top = jnp.broadcast_to(top, (block, LANES))
+        f_ref[rows, :] = top
+        note(0, g, top)
+
+    def exponents(g, carry):
+        rows = pl.ds(pl.multiple_of(g * block, block), block)
+        top = f_ref[rows, :]
         total = jnp.zeros((block, LANES), jnp.float32)
         for c in range(tiles):
             e = jnp.exp(e_ref[c, rows, :] - top)
             e_ref[c, rows, :] = e
             total = total + e
-        total = jnp.broadcast_to(jnp.sum(total, axis=1, keepdims=True), (block, LANES))
-        for i, value in enumerate((top, total)):
-            picked = jnp.where(diagonal, value, 0.0)
-            stat[0, i, pl.ds(g, 1), :] = jnp.sum(picked, axis=0, keepdims=True)
+        f_ref[rows, :] = total
         return carry
 
-    lax.fori_loop(0, ext // block, finish, 0)
+    lax.fori_loop(0, ext // block, exponents, 0)
+
+    for g in range(ext // block):
+        total = jnp.sum(f_ref[pl.ds(g * block, block), :], axis=1, keepdims=True)
+        note(1, g, jnp.broadcast_to(total, (block, LANES)))
 
     def stat_copy(k):
         bit = lax.rem(y // (1 << k), 2)
@@ -372,16 +408,13 @@
         )
     stat[rounds, 1] = jnp.exp(stat[0, 0] - stat[rounds, 0]) / stat[rounds, 1]
 
-    def widen(g, carry):
-        rows = pl.ds(pl.multiple_of(g * block, block), block)
-        row = jnp.broadcast_to(stat[rounds, 1, pl.ds(g, 1), :], (block, LANES))
+    for g in range(ext // block):
+        rows = pl.ds(g * block, block)
+        row = jnp.broadcast_to(stat[rounds, 1, g : g + 1, :], (block, LANES))
         factor = jnp.sum(jnp.where(diagonal, row, 0.0), axis=1, keepdims=True)
         factor = jnp.broadcast_to(factor, (block, LANES))
-        valid = valid_ref[pl.ds(pl.multiple_of(g * block, block) + rim, block), :] > 0
+        valid = valid_ref[pl.ds(g * block + rim, block), :] > 0
         f_ref[rows, :] = jnp.where(valid, factor, -1.0)
-        return carry
-
-    lax.fori_loop(0, ext // block, widen, 0)
 
     def map_gradient(c):
         first = (lane + c * chunk).astype(jnp.float32)
@@ -591,24 +624,29 @@
     stages, last = plan(hop, rate, spread_out, gather_in, exchange, None)
     k_stages, k_last = plan(tap_hop, 1, k_spread, k_gather, k_exchange, k_take)
     begun = 2 * count
-    steps = begun + max((last + rate - 1) // rate, k_last)
+    f_end = max(begun + 4, count + peers * f_tiles)
+    steps = max(begun + (last + rate - 1) // rate, begun + k_last, f_end + 1)
 
     def step(s, carry):
         @pl.when(s < count)
         def _():
             produce(s)
 
-        @pl.when(s == count)
-        def _():
+        c = s - count
+
+        @pl.when((c >= 0) & (c < peers * f_tiles))
+        def _():
+            p = lax.rem(y + 1 + c // f_tiles, peers)
+            f_compute(p, lax.rem(c, f_tiles))
+
             for d in range(1, peers):
-                f_compute(lax.rem(y + d, peers))
-                f_copy(d).start()
-
-        @pl.when(s == begun)
-        def _():
-            f_compute(y)
-
-        c = s - count
+                @pl.when(c // f_tiles == d - 1)
+                def _(d=d):
+                    f_copy(d, lax.rem(c, f_tiles)).start()
+
+        @pl.when(s == f_end)
+        def _():
+            f_finish()
 
         @pl.when((c >= 0) & (c < count))
         def _():
@@ -636,15 +674,6 @@
         return carry
 
     lax.fori_loop(0, steps, step, 0)
-
-    for d in range(1, peers):
-        f_copy(d).wait_recv()
-    total = fpart[y]
-    for d in range(1, peers):
-        total = total + fin[d - 1]
-    gf_ref[...] = (total * scale).astype(gf_ref.dtype)
-    for d in range(1, peers):
-        f_copy(d).wait_send()
 
     @pl.when(jnp.logical_not(is_end))
     def _():
@@ -677,6 +706,7 @@
 HOP = 3
 TAP_HOP = 3
 PARTS = 2
+BATCH = 4
 
 
 def gradients(labels, lengths, frame_rows, queries, kernel, scale):
@@ -731,10 +761,11 @@
         vmem((9, wide // 4, chunk), f32),
         vmem((9 * (taps // 4 + 1), 8, chunk), f32),
         vmem((32 * SPAN, chunk), f32),
+        vmem((2, 2 * rim, width), jnp.bfloat16),
     ]
     dma = pltpu.SemaphoreType.DMA
-    scratch += [dma((bits, subs))] * 2 + [dma((subs,))] * 4 + [dma((peers - 1,))] * 2
-    scratch += [dma((2, 2))] * 2 + [dma((rounds,))] * 2 + [dma((4,)), dma((PARTS,))]
+    scratch += [dma((bits, subs))] * 2 + [dma((subs,))] * 4 + [dma((peers - 1, row_count // LANES))] * 2
+    scratch += [dma((2, 2))] * 2 + [dma((rounds,))] * 2 + [dma((6,)), dma((PARTS,))]
     scratch += [dma((bits, pairs))] * 2 + [dma((pairs,))] * 6
     hbm = pl.BlockSpec(memory_space=pl.ANY)
     dims = (tms, peers, recs, chunk, sub, HOP, TAP_HOP)

time: 101 us -> 95.4 us (0.945)
  Pallas kernels: 99.8 us -> 93.9 us
    pallas_call x1, Pallas kernels: 98.5 us -> 92.6 us  [gradients(): pl.pallas_call(functools.partial(gradient_kernel, dims, scale), out_shape...]
where the time goes in v3:
time: 95.4 us; the launch traced here: 95.2 us
  Pallas kernels  93.9 us (98%)
  between operations  1.29 us (1%)
    pallas_call x1, Pallas kernels, gradients(): pl.pallas_call(functools.partial(gradient_kernel, dims, scale), out_shape...  92.6 us

profile of v3, /device:TPU:0, one launch (start us, length us, event | category | flops | bytes accessed | tf_op | source)
XLA Modules:
  0.0 95.2 jit_solution(6038545860608061976)
XLA Ops:
  1.3 92.6 %gradients.1 = (bf16[512,512]{1,0:T(8,128)(2,1)S(1)}, bf16[2048,256]{1,0:T(8,128)(2,1)S(1)}, f32[33,2048]{1,0:T(8,128)S(1)}) custom-call(s32[1,512]{1,0:T(1,128)} %lab_hbm.1, s32[1]{0:T(128)S(6)} %copy.8.len_hbm, bf16[512,1024]{1,0:T(8,128)(2,1)} %bitcast.2, bf16[2048,1024]{1,0:T(8,128)(2,1)} %qu_hbm.1, f32[33,2048]{1,0:T(8,128)} %kern_hbm.1), custom_call_target="tpu_custom_call" | custom-call | tf_op jit(solution)/shard_map/gradients/pallas_call | solution.py:772
  93.9 1.3 %store.1 = (bf16[512,512]{1,0:T(8,128)(2,1)}, bf16[2048,256]{1,0:T(8,128)(2,1)}, f32[33,2048]{1,0:T(8,128)}) custom-call(bf16[512,512]{1,0:T(8,128)(2,1)S(1)} %get-tuple-element.9.refs_0_, bf16[2048,256]{1,0:T(8,128)(2,1)S(1)} %get-tuple-element.10.refs_1_, f32[33,2048]{1,0:T(8,128)S(1)} %get-tuple-element.11.refs_2_), custom_call_target="tpu_custom_call" | custom-call | tf_op jit(solution)/shard_map/store/pallas_call | solution.py:799

commit v4 on v3

--- a/solution.py
+++ b/solution.py
@@ -98,18 +98,19 @@
 
 
 def bit_reversed(p, bits):
-    return sum(((p >> k) & 1) << (bits - 1 - k) for k in range(bits))
+    return sum((p // (1 << k)) % 2 * (1 << (bits - 1 - k)) for k in range(bits))
 
 
 def gradient_kernel(dims, scale, lab_hbm, len_hbm, fr_hbm, qu_hbm, kern_hbm, *refs):
-    tms, peers, recs, chunk, sub, hop, tap_hop = dims
+    tms, peers, recs, chunk, runs, hop, tap_hop = dims
     bits = recs.bit_length() - 1
     gf_ref, gq_ref, gk_ref = refs[:3]
     scratch = refs[3:]
     acc, scratch = scratch[:bits], scratch[bits:]
     arrived, scratch = scratch[:bits], scratch[bits:]
-    kacc, ksum, karrived, scratch = (scratch[0], scratch[1], scratch[2], scratch[3:])
-    (mid, outer, inner, kmid, kouter, kinner, kgot, fpart, fin, sg_ref, grad) = scratch[:11]
+    kacc, scratch = scratch[:bits], scratch[bits:]
+    karrived, scratch = scratch[:bits], scratch[bits:]
+    (mid, outer, inner, kmid, kouter, kinner, kfin, fpart, fin, sg_ref, grad) = scratch[:11]
     (sc_ref, e_ref, f_ref, lab_ref, valid_ref, xh_ref, hin, hout, stat, stat_in) = scratch[11:21]
     (fr_ref, qu_ref, kern_ref, lab_row, lab_in, len_ref, strm_ref, filt_ref, turn) = scratch[21:30]
     edge_ref, scratch = scratch[30], scratch[31:]
@@ -171,9 +172,7 @@
     loads[3].start()
 
     count = queries // chunk
-    subs = queries // sub
-    per = chunk // sub
-    rate = per // 2
+    per = chunk // runs[0][2]
     cols = width // recs
     fcols = width // peers
     row_count = sg_ref.shape[0]
@@ -200,8 +199,8 @@
     def at(c):
         return pl.ds(pl.multiple_of(c * chunk, chunk), chunk)
 
-    def sub_at(j):
-        return pl.ds(pl.multiple_of(j * sub, sub), sub)
+    def sub_at(row, size):
+        return pl.ds(pl.multiple_of(row, size), size)
 
     def f_rows(i):
         return pl.ds(pl.multiple_of(i * LANES, LANES), LANES)
@@ -462,37 +461,36 @@
         zero = jnp.zeros((8, LANES), jnp.float32)
         sums = lax.fori_loop(0, row_count // block, body, (zero,) * taps_n)
         for j in range(taps_n):
-            kacc[c, j : j + 1, :] = jnp.sum(sums[j], axis=0, keepdims=True)
-
-    def rec_copy(k, j):
-        n = recs >> k
+            total = jnp.sum(sums[j], axis=0, keepdims=True)
+            kacc[0][c // recs, bit_reversed(c % recs, bits), j : j + 1, :] = total
+
+    def rec_copy(k, m):
+        n, rows = recs >> k, sub_at(m[1], m[2])
         theirs = (1 - my_bits[k]) * (n // 2)
         return copy(
-            acc[k].at[pl.ds(theirs, n // 2), sub_at(j)],
-            arrived[k].at[:, sub_at(j)],
-            rec_send.at[k, j],
-            rec_recv.at[k, j],
+            acc[k].at[pl.ds(theirs, n // 2), rows],
+            arrived[k].at[:, rows],
+            rec_send.at[k, m[0]],
+            rec_recv.at[k, m[0]],
             {"rec": rec_peers[k]},
         )
 
-    def summed(k, j):
-        rec_copy(k, j).wait_recv()
-        n = recs >> k
+    def summed(k, m):
+        rec_copy(k, m).wait_recv()
+        n, rows = recs >> k, sub_at(m[1], m[2])
         mine = my_bits[k] * (n // 2)
-        return acc[k][pl.ds(mine, n // 2), sub_at(j), :] + arrived[k][:, sub_at(j), :]
-
-    def inward_copy(j, to_mid):
+        return acc[k][pl.ds(mine, n // 2), rows, :] + arrived[k][:, rows, :]
+
+    def inward_copy(m, to_mid):
+        rows = sub_at(m[1], m[2])
         big = inner if to_mid else outer
         recv = inn_recv if to_mid else out_recv
-        return copy(mid.at[sub_at(j)], big.at[sub_at(j)], in_send.at[j], recv.at[j], {"tm": inward})
-
-    def outward_copy(j):
+        return copy(mid.at[rows], big.at[rows], in_send.at[m[0]], recv.at[m[0]], {"tm": inward})
+
+    def outward_copy(m):
+        rows = sub_at(m[1], m[2])
         return copy(
-            inner.at[sub_at(j)],
-            inner.at[sub_at(j)],
-            out_send.at[j],
-            inn_recv.at[j],
-            {"tm": outward},
+            inner.at[rows], inner.at[rows], out_send.at[m[0]], inn_recv.at[m[0]], {"tm": outward}
         )
 
     def produce(c):
@@ -507,53 +505,73 @@
         for p in range(recs):
             j = bit_reversed(p, bits)
             acc[0][p, at(c), :] = part[:, j * cols : (j + 1) * cols]
-        for h in range(per):
-            rec_copy(0, c * per + h).start()
-
-    def exchange(k, j):
-        acc[k][:, sub_at(j), :] = summed(k - 1, j)
-        rec_copy(k, j).start()
-
-    def gather_in(j):
-        mid[sub_at(j), :] = summed(bits - 1, j)[0]
+
+        @pl.when(c < count - 1)
+        def _():
+            for h in range(per):
+                first = c * per + h
+                rec_copy(0, (first, first * runs[0][2], runs[0][2])).start()
+
+        @pl.when(c == count - 1)
+        def _():
+            for index, row, size, number in runs:
+                for h in range(number):
+                    if row + h * size >= queries - chunk:
+                        rec_copy(0, (index + h, row + h * size, size)).start()
+
+    def exchange(k, m):
+        acc[k][:, sub_at(m[1], m[2]), :] = summed(k - 1, m)
+        rec_copy(k, m).start()
+
+    def gather_in(m):
+        rows = sub_at(m[1], m[2])
+        mid[rows, :] = summed(bits - 1, m)[0]
 
         @pl.when(jnp.logical_not(is_end))
         def _():
-            inward_copy(j, False).wait_recv()
-            mid[sub_at(j), :] += outer[sub_at(j), :]
+            inward_copy(m, False).wait_recv()
+            mid[rows, :] += outer[rows, :]
 
         @pl.when(is_mid)
         def _():
-            inward_copy(j, True).start()
+            inward_copy(m, True).start()
 
         @pl.when(jnp.logical_not(is_mid))
         def _():
-            inward_copy(j, False).start()
-
-    def spread_out(j):
-        inward_copy(j, True).wait_recv()
+            inward_copy(m, False).start()
+
+    def spread_out(m):
+        rows = sub_at(m[1], m[2])
+        inward_copy(m, True).wait_recv()
 
         @pl.when(is_mid)
         def _():
-            inner[sub_at(j), :] += mid[sub_at(j), :]
+            inner[rows, :] += mid[rows, :]
 
         @pl.when(jnp.logical_not(is_end))
         def _():
-            outward_copy(j).start()
-
-        gq_ref[sub_at(j), :] = (inner[sub_at(j), :] * scale).astype(gq_ref.dtype)
+            outward_copy(m).start()
+
+        gq_ref[rows, :] = (inner[rows, :] * scale).astype(gq_ref.dtype)
         for k in range(bits):
-            rec_copy(k, j).wait_send()
-        inward_copy(j, False).wait_send()
+            rec_copy(k, m).wait_send()
+        inward_copy(m, False).wait_send()
 
     def k_copy(k, i):
-        src = kacc.at[2 * i + 1 - my_bits[0]] if k == 0 else ksum.at[k - 1, i]
-        return copy(src, karrived.at[k, i], k_send.at[k, i], k_recv.at[k, i], {"rec": rec_peers[k]})
+        n = recs >> k
+        theirs = (1 - my_bits[k]) * (n // 2)
+        return copy(
+            kacc[k].at[i, pl.ds(theirs, n // 2)],
+            karrived[k].at[i],
+            k_send.at[k, i],
+            k_recv.at[k, i],
+            {"rec": rec_peers[k]},
+        )
 
     def k_summed(k, i):
         k_copy(k, i).wait_recv()
-        own = kacc[2 * i + my_bits[0]] if k == 0 else ksum[k - 1, i]
-        return own + karrived[k, i]
+        n = recs >> k
+        return kacc[k][i, pl.ds(my_bits[k] * (n // 2), n // 2)] + karrived[k][i]
 
     def k_inward(i, to_mid):
         dst = kinner if to_mid else kouter
@@ -563,15 +581,25 @@
     def k_outward(i):
         return copy(kinner.at[i], kinner.at[i], kout_send.at[i], kinn_recv.at[i], {"tm": outward})
 
-    def k_give(i):
-        return copy(kinner.at[i], kgot.at[i], kg_send.at[i], kg_recv.at[i], {"rec": rec_peers[0]})
+    place = sum(my_bits[k] * (recs >> (k + 1)) for k in range(bits))
+
+    def k_give(k, i):
+        n = recs >> (k + 1)
+        rows = pl.ds(place // n * n, n)
+        return copy(
+            kfin.at[i, rows],
+            kfin.at[i, rows],
+            kg_send.at[k, i],
+            kg_recv.at[k, i],
+            {"rec": rec_peers[k]},
+        )
 
     def k_exchange(k, i):
-        ksum[k - 1, i] = k_summed(k - 1, i)
+        kacc[k][i] = k_summed(k - 1, i)
         k_copy(k, i).start()
 
     def k_gather(i):
-        kmid[i] = k_summed(bits - 1, i)
+        kmid[i] = k_summed(bits - 1, i)[0]
 
         @pl.when(jnp.logical_not(is_end))
         def _():
@@ -593,20 +621,23 @@
         def _():
             kinner[i] += kmid[i]
 
-        k_give(i).start()
-
         @pl.when(jnp.logical_not(is_end))
         def _():
             k_outward(i).start()
 
-        gk_ref[:, at(2 * i + my_bits[0])] = kinner[i]
+        kfin[i, place] = kinner[i]
+        k_give(bits - 1, i).start()
         for k in range(bits):
             k_copy(k, i).wait_send()
         k_inward(i, False).wait_send()
 
-    def k_take(i):
-        k_give(i).wait_recv()
-        gk_ref[:, at(2 * i + 1 - my_bits[0])] = kgot[i]
+    def k_take(k, i):
+        k_give(k, i).wait_recv()
+        if k > 0:
+            k_give(k - 1, i).start()
+        else:
+            for p in range(recs):
+                gk_ref[:, at(i * recs + p)] = kfin[i, bit_reversed(p, bits)]
 
     reach = half - 1
     away = jnp.where(low, reach - t, t - half)
@@ -614,18 +645,29 @@
     def plan(step, first, spread, gather, swap, take):
         base = first + (bits - 1) * step
         ends = base + 2 * step * reach + step
-        late = [(ends + first, take)] if take else []
+        late = [
+            (ends + (bits - 1 - k) * step + (step if k else first), functools.partial(take, k))
+            for k in range(bits if take else 0)
+        ]
         late += [(base + step * (reach + away + 1), spread), (base + step * (reach - away), gather)]
         late += [
             (first + (k - 1) * step, functools.partial(swap, k)) for k in range(bits - 1, 0, -1)
         ]
-        return late, ends + (first if take else 0)
-
-    stages, last = plan(hop, rate, spread_out, gather_in, exchange, None)
+        return late, ends + ((bits - 1) * step + first if take else 0)
+
+    stages, last = plan(hop, 1, spread_out, gather_in, exchange, None)
     k_stages, k_last = plan(tap_hop, 1, k_spread, k_gather, k_exchange, k_take)
     begun = 2 * count
-    f_end = max(begun + 4, count + peers * f_tiles)
-    steps = max(begun + (last + rate - 1) // rate, begun + k_last, f_end + 1)
+    quads = count // recs
+    made = lambda c: c + 1 + max(c + 1 - f_tiles, 0) // 2
+    gap = next(
+        x for x in range(1, recs + 1) if all(made(x * q) >= recs * q for q in range(1, quads + 1))
+    )
+    k_stages = k_stages + [(0, lambda i: k_copy(0, i).start())]
+    f_own = max(begun, count + (peers - 1) * f_tiles)
+    f_end = f_own + f_tiles
+    messages = runs[-1][0] + runs[-1][3]
+    steps = max(messages + last, count + 1 + gap * quads + k_last, f_end + 1)
 
     def step(s, carry):
         @pl.when(s < count)
@@ -634,15 +676,19 @@
 
         c = s - count
 
-        @pl.when((c >= 0) & (c < peers * f_tiles))
-        def _():
-            p = lax.rem(y + 1 + c // f_tiles, peers)
-            f_compute(p, lax.rem(c, f_tiles))
+        @pl.when((c >= 0) & (c < (peers - 1) * f_tiles))
+        def _():
+            i = c % f_tiles
+            f_compute(lax.rem(y + 1 + c // f_tiles, peers), i)
 
             for d in range(1, peers):
                 @pl.when(c // f_tiles == d - 1)
                 def _(d=d):
-                    f_copy(d, lax.rem(c, f_tiles)).start()
+                    f_copy(d, i).start()
+
+        @pl.when((s >= f_own) & (s < f_own + f_tiles))
+        def _():
+            f_compute(y, s - f_own)
 
         @pl.when(s == f_end)
         def _():
@@ -650,26 +696,28 @@
 
         @pl.when((c >= 0) & (c < count))
         def _():
-            tap_gradient(c)
-
-            @pl.when(lax.rem(c, 2) == 1)
-            def _():
-                k_copy(0, c // 2).start()
-
-        for i in range(rate):
-            for delay, stage in stages:
-                tick = s * rate + i - delay
-
-                @pl.when((tick >= 0) & (tick < subs))
-                def _(stage=stage, tick=tick):
-                    stage(tick)
+            def tap(i, carry):
+                tap_gradient(i)
+                return carry
+
+            begin = c + jnp.maximum(c - f_tiles, 0) // 2
+            end = c + 1 + jnp.maximum(c + 1 - f_tiles, 0) // 2
+            lax.fori_loop(jnp.minimum(begin, count), jnp.minimum(end, count), tap, 0)
+
+        for delay, stage in stages:
+            for index, row, size, number in runs:
+                tick = s - delay - index
+
+                @pl.when((tick >= 0) & (tick < number))
+                def _(stage=stage, tick=tick, index=index, row=row, size=size):
+                    stage((index + tick, row + tick * size, size))
 
         for delay, stage in k_stages:
             tick = c - delay
 
-            @pl.when((tick >= 0) & (tick < count) & (lax.rem(tick + 2, 2) == 1))
+            @pl.when((tick >= gap) & (tick <= gap * quads) & (lax.rem(tick + gap * steps, gap) == 0))
             def _(stage=stage, tick=tick):
-                stage(tick // 2)
+                stage(tick // gap - 1)
 
         return carry
 
@@ -677,14 +725,16 @@
 
     @pl.when(jnp.logical_not(is_end))
     def _():
-        def drain(j, carry):
-            outward_copy(j).wait_send()
-            return carry
-
-        lax.fori_loop(0, subs, drain, 0)
+        for index, row, size, number in runs:
+            def drain(h, carry, index=index, row=row, size=size):
+                outward_copy((index + h, row + h * size, size)).wait_send()
+                return carry
+
+            lax.fori_loop(0, number, drain, 0)
 
     def k_drain(i, carry):
-        k_give(i).wait_send()
+        for k in range(bits):
+            k_give(k, i).wait_send()
 
         @pl.when(jnp.logical_not(is_end))
         def _():
@@ -692,7 +742,7 @@
 
         return carry
 
-    lax.fori_loop(0, count // 2, k_drain, 0)
+    lax.fori_loop(0, count // recs, k_drain, 0)
     for k in range(rounds):
         stat_copy(k).wait_send()
     for side in range(2):
@@ -702,7 +752,22 @@
                 one.wait_send()
 
 
-SPLIT = 2
+PIECE = 64
+TAIL = (64, 64)
+
+
+def message_runs(queries):
+    runs, row, index = [], 0, 0
+    body = (queries - sum(TAIL)) // PIECE
+    for size, number in [(PIECE, body)] + [(size, 1) for size in TAIL]:
+        if runs and runs[-1][2] == size:
+            runs[-1] = runs[-1][:3] + (runs[-1][3] + number,)
+        else:
+            runs.append((index, row, size, number))
+        index, row = index + number, row + size * number
+    return tuple(runs)
+
+
 HOP = 3
 TAP_HOP = 3
 PARTS = 2
@@ -716,27 +781,24 @@
     query_count = queries.shape[0]
     taps = kernel.shape[0]
     chunk = LANES
-    sub = chunk // SPLIT
+    runs = message_runs(query_count)
+    messages = runs[-1][0] + runs[-1][3]
     count = query_count // chunk
-    subs = query_count // sub
     cols, fcols = (width // recs, width // peers)
     rim = taps // 2
     ext, wide = (row_count + 2 * rim, row_count + 4 * rim)
     rounds = peers.bit_length() - 1
     stat_rows = (ext // (8 * GROUPS) + 7) // 8 * 8
-    pairs = count // 2
+    quads = count // recs
     f32 = jnp.float32
     vmem = pltpu.VMEM
-    small = vmem((pairs, taps, chunk), f32)
+    small = vmem((quads, taps, chunk), f32)
     block = vmem((query_count, cols), f32)
     scratch = [vmem((recs >> k, query_count, cols), f32) for k in range(bits)]
     scratch += [vmem((recs >> (k + 1), query_count, cols), f32) for k in range(bits)]
-    scratch += [
-        vmem((count, taps, chunk), f32),
-        vmem((max(bits - 1, 1), pairs, taps, chunk), f32),
-        vmem((bits, pairs, taps, chunk), f32),
-    ]
-    scratch += [block] * 3 + [small] * 4
+    scratch += [vmem((quads, recs >> k, taps, chunk), f32) for k in range(bits)]
+    scratch += [vmem((quads, recs >> (k + 1), taps, chunk), f32) for k in range(bits)]
+    scratch += [block] * 3 + [small] * 3 + [vmem((quads, recs, taps, chunk), f32)]
     scratch += [
         vmem((peers, row_count, fcols), f32),
         vmem((peers - 1, row_count, fcols), f32),
@@ -764,11 +826,11 @@
         vmem((2, 2 * rim, width), jnp.bfloat16),
     ]
     dma = pltpu.SemaphoreType.DMA
-    scratch += [dma((bits, subs))] * 2 + [dma((subs,))] * 4 + [dma((peers - 1, row_count // LANES))] * 2
+    scratch += [dma((bits, messages))] * 2 + [dma((messages,))] * 4 + [dma((peers - 1, row_count // LANES))] * 2
     scratch += [dma((2, 2))] * 2 + [dma((rounds,))] * 2 + [dma((6,)), dma((PARTS,))]
-    scratch += [dma((bits, pairs))] * 2 + [dma((pairs,))] * 6
+    scratch += [dma((bits, quads))] * 2 + [dma((quads,))] * 4 + [dma((bits, quads))] * 2
     hbm = pl.BlockSpec(memory_space=pl.ANY)
-    dims = (tms, peers, recs, chunk, sub, HOP, TAP_HOP)
+    dims = (tms, peers, recs, chunk, runs, HOP, TAP_HOP)
     return pl.pallas_call(
         functools.partial(gradient_kernel, dims, scale),
         out_shape=(

time: 95.4 us -> 94.5 us (level)
  no operation moved by 1% of the time
where the time goes in v4:
time: 94.5 us; the launch traced here: 94.4 us
  Pallas kernels  93.1 us (99%)
  between operations  1.29 us (1%)
    pallas_call x1, Pallas kernels, gradients(): pl.pallas_call(functools.partial(gradient_kernel, dims, scale), out_shape...  91.8 us

profile of v4, /device:TPU:0, one launch (start us, length us, event | category | flops | bytes accessed | tf_op | source)
XLA Modules:
  0.0 94.4 jit_solution(279667976478429475)
XLA Ops:
  1.3 91.8 %gradients.1 = (bf16[512,512]{1,0:T(8,128)(2,1)S(1)}, bf16[2048,256]{1,0:T(8,128)(2,1)S(1)}, f32[33,2048]{1,0:T(8,128)S(1)}) custom-call(s32[1,512]{1,0:T(1,128)} %lab_hbm.1, s32[1]{0:T(128)S(6)} %copy.8.len_hbm, bf16[512,1024]{1,0:T(8,128)(2,1)} %bitcast.2, bf16[2048,1024]{1,0:T(8,128)(2,1)} %qu_hbm.1, f32[33,2048]{1,0:T(8,128)} %kern_hbm.1), custom_call_target="tpu_custom_call" | custom-call | tf_op jit(solution)/shard_map/gradients/pallas_call | solution.py:834
  93.1 1.3 %store.1 = (bf16[512,512]{1,0:T(8,128)(2,1)}, bf16[2048,256]{1,0:T(8,128)(2,1)}, f32[33,2048]{1,0:T(8,128)}) custom-call(bf16[512,512]{1,0:T(8,128)(2,1)S(1)} %get-tuple-element.9.refs_0_, bf16[2048,256]{1,0:T(8,128)(2,1)S(1)} %get-tuple-element.10.refs_1_, f32[33,2048]{1,0:T(8,128)S(1)} %get-tuple-element.11.refs_2_), custom_call_target="tpu_custom_call" | custom-call | tf_op jit(solution)/shard_map/store/pallas_call | solution.py:861
